TPU v7x, 32 devices: a whole 2x2x4 slice. The times are simulated.
32 devices in a mesh: radial: 1, mode: 32 (over z, y, x, core).
Axes of the slice: x: 2, y: 2, z: 4, core: 2. Of those that a mesh axis runs over, the one named last changes fastest.
Arguments:
- spectral_state: float32 [64, 3, 2, 2, 129], P('mode', None, 'radial'), may hold values from -6 to 6
- synthesis_table: bfloat16 [64, 129, 128], P('mode', None, 'radial'), may hold values from -0.03125 to 0.03125
- low_orders: int32 [64], replicated, may hold values from 0 to 63, each once
- diffusion: float32 [3], replicated, may hold values from 200 to 2000
- coupling: float32 [3], replicated, may hold values from 1 to 4
Outputs:
- updated: float32 [64, 3, 2, 2, 129], P('mode', None, 'radial')
Inputs may be any that keep to these rules, and one draw needn't show every extreme that they name: A permutation: pair j holds the orders low_orders[j] and 127 - low_orders[j].
All inputs are finite; a program needn't handle non-finite values.
Results may differ from a plain program's by a relative error of at most 0.0023.
The roundings to bfloat16 on the way count: a program that leaves them out, or rounds other values in their place, can miss the bound.
Values may be sent and summed in bfloat16 or wider, within the bound.
No kernel may reach another device: no remote copies, remote signals or barrier semaphores. Data moves between devices by JAX's collectives and lax.ppermute only.
A program may use at most 64 MiB of HBM per device.

v0:
```python
import math

import jax
import jax.numpy as jnp
from jax import lax
from jax.sharding import PartitionSpec as P

inner_radius = 0.538
shell_step = 1.0 / 2048.0
block_limit = 384


def with_halo(shard, sides, width):
    for axis, dim in sides:
        count, length = (lax.axis_size(axis), shard.shape[dim])
        up = [(i, (i + 1) % count) for i in range(count - 1)]
        down = [(j, i) for i, j in up]
        last = lax.slice_in_dim(shard, length - width, length, axis=dim)
        first = lax.slice_in_dim(shard, 0, width, axis=dim)
        before = lax.ppermute(last, axis, up)
        after = lax.ppermute(first, axis, down)
        shard = jnp.concatenate([before, shard, after], axis=dim)
    return shard


def pair_layout(lower_orders, rows_total):
    orders_total = rows_total - 1
    row_index = lax.iota(jnp.int32, rows_total)[None, :]
    lower_col = lower_orders[:, None]
    in_lower = row_index < orders_total - lower_col
    degree = jnp.where(in_lower, lower_col + row_index, row_index - 1)
    order_of = jnp.where(in_lower, lower_col, orders_total - 1 - lower_col)
    return (in_lower, degree, order_of)


def body(spectral_state, synthesis_table, low_orders, diffusion, coupling):
    synthesis_table = lax.all_gather(synthesis_table, "radial", axis=2, tiled=True)
    pairs_dev, field_count, shell_count, part_count, rows_total = spectral_state.shape
    half_lat = synthesis_table.shape[2]
    lat_total = 2 * half_lat
    orders_total = rows_total - 1
    lon_total = 3 * orders_total
    mode_count = lax.axis_size("mode")
    column_count = 4 * pairs_dev * mode_count
    own_lower = lax.dynamic_slice_in_dim(low_orders, lax.axis_index("mode") * pairs_dev, pairs_dev)
    in_lower, degree, order_of = pair_layout(own_lower, rows_total)
    parity_even = (degree + order_of) % 2 == 0
    order_mask = jnp.stack([in_lower, jnp.logical_not(in_lower)], axis=1)
    parity_mask = jnp.stack([parity_even, jnp.logical_not(parity_even)], axis=1)
    row_sign = jnp.where(parity_even, 1.0, -1.0).astype(jnp.float32)
    order_float = order_mask.astype(jnp.float32)
    coeffs = spectral_state.astype(jnp.bfloat16)
    all_lower = low_orders.reshape(mode_count, 1, pairs_dev, 1)
    partner = jnp.arange(2, dtype=jnp.int32).reshape(1, 1, 1, 2)
    column_order = jnp.where(partner == 0, all_lower, orders_total - 1 - all_lower)
    column_order = jnp.broadcast_to(column_order, (mode_count, 2, pairs_dev, 2)).reshape(
        column_count
    )
    cosine_rows = jnp.broadcast_to(
        jnp.arange(2, dtype=jnp.int32).reshape(1, 2, 1, 1) == 0, (mode_count, 2, pairs_dev, 2)
    ).reshape(column_count)
    synth_weight = jnp.where(column_order == 0, 1.0, 2.0).astype(jnp.float32)
    block_size = min(block_limit, lon_total)
    block_total = lon_total // block_size
    analysis_scale = 2.0 * math.sqrt(orders_total * rows_total / (lat_total * lon_total))
    spread = (
        coeffs[:, None, :, :, :, None, :]
        * parity_mask.astype(jnp.bfloat16)[:, :, None, None, None, None, :]
        * order_mask.astype(jnp.bfloat16)[:, None, None, None, None, :, :]
    )
    halves = jnp.einsum(
        "pqfsckr,prn->qnsfcpk", spread, synthesis_table, preferred_element_type=jnp.float32
    )
    northern = halves[0] + halves[1]
    southern = (halves[0] - halves[1])[::-1]
    joined = jnp.concatenate([northern, southern], axis=0).astype(jnp.bfloat16)
    pieces = lax.all_to_all(
        joined.reshape(lat_total, shell_count, coeffs.shape[1], 4 * pairs_dev),
        "mode",
        split_axis=0,
        concat_axis=3,
        tiled=True,
    )
    lat_dev = pieces.shape[0]
    item_count = pieces.shape[1]
    row_total = lat_dev * item_count * field_count
    weighted = pieces.reshape(row_total, column_count).astype(jnp.float32) * synth_weight[None, :]
    totals = jnp.zeros((row_total, column_count), jnp.float32)
    for block_at in range(block_total):
        longitude = block_at * block_size + lax.iota(jnp.int32, block_size)
        phase_index = column_order[:, None] * longitude[None, :] % lon_total
        angles = phase_index.astype(jnp.float32) * (2.0 * math.pi / lon_total)
        wave_table = jnp.where(cosine_rows[:, None], jnp.cos(angles), -jnp.sin(angles))
        values = jnp.dot(weighted, wave_table, precision=lax.Precision.HIGHEST)
        values = values.reshape(lat_dev, item_count, field_count, block_size)
        products = jnp.stack(
            [
                values[:, :, 0] * values[:, :, 1],
                values[:, :, 0] * values[:, :, 2],
                values[:, :, 1] * values[:, :, 2],
            ],
            axis=2,
        )
        totals = totals + lax.dot_general(
            products.reshape(row_total, block_size),
            wave_table,
            (((1,), (1,)), ((), ())),
            precision=lax.Precision.HIGHEST,
        )
    answers = (totals * analysis_scale).astype(jnp.bfloat16)
    returned = lax.all_to_all(
        answers.reshape(lat_dev, item_count, field_count, column_count),
        "mode",
        split_axis=3,
        concat_axis=0,
        tiled=True,
    )
    subset_fields = returned.shape[2]
    arranged = returned.reshape(lat_total, shell_count, subset_fields, part_count, pairs_dev, 2)
    from_north = jnp.einsum(
        "prn,nsfcpk->pkfscr",
        synthesis_table,
        arranged[:half_lat],
        preferred_element_type=jnp.float32,
    )
    from_south = jnp.einsum(
        "prn,nsfcpk->pkfscr",
        synthesis_table,
        arranged[half_lat:][::-1],
        preferred_element_type=jnp.float32,
    )
    combined = from_north + row_sign[:, None, None, None, None, :] * from_south
    nonlinear = jnp.sum(combined * order_float[:, :, None, None, None, :], axis=1)
    radial_at = lax.axis_index("radial")
    rate_col = diffusion.reshape(1, field_count, 1, 1)
    strength = coupling.reshape(1, field_count, 1, 1)
    degree_term = degree.astype(jnp.float32)
    degree_term = (degree_term * (degree_term + 1.0))[:, None, None, :] * (shell_step * shell_step)
    with_edges = with_halo(spectral_state.astype(jnp.bfloat16), (("radial", 2),), 1).astype(
        spectral_state.dtype
    )
    diagonals = []
    drives = []
    for shell_at in range(shell_count):
        radius = (
            inner_radius
            + ((radial_at * shell_count + shell_at).astype(jnp.float32) + 0.5) * shell_step
        )
        damping = degree_term / (radius * radius)
        middle = with_edges[:, :, shell_at + 1]
        laplace = (
            with_edges[:, :, shell_at + 2]
            - 2.0 * middle
            + with_edges[:, :, shell_at]
            - damping * middle
        )
        drives.append(middle + rate_col * (laplace + strength * nonlinear[:, :, shell_at]))
        diagonals.append(1.0 + rate_col * (2.0 + damping))
    narrow_zero = jnp.zeros(diagonals[0].shape, jnp.float32)
    wide_zero = jnp.zeros(drives[0].shape, jnp.float32)
    pivot_prev = narrow_zero
    carry_u, carry_v, carry_w = (wide_zero, narrow_zero, narrow_zero)
    pivots, sweep_u, sweep_v, sweep_w = ([], [], [], [])
    for shell_at in range(shell_count):
        denom_at = diagonals[shell_at] + rate_col * pivot_prev
        pivot_prev = -rate_col / denom_at
        first_drive = rate_col if shell_at == 0 else 0.0
        last_drive = rate_col if shell_at == shell_count - 1 else 0.0
        carry_u = (drives[shell_at] + rate_col * carry_u) / denom_at
        carry_v = (first_drive + rate_col * carry_v) / denom_at
        carry_w = (last_drive + rate_col * carry_w) / denom_at
        pivots.append(pivot_prev)
        sweep_u.append(carry_u)
        sweep_v.append(carry_v)
        sweep_w.append(carry_w)
    solved_u, solved_v, solved_w = ([sweep_u[-1]], [sweep_v[-1]], [sweep_w[-1]])
    shell_at = 0
    solved_u.insert(0, sweep_u[shell_at] - pivots[shell_at] * solved_u[0])
    solved_v.insert(0, sweep_v[shell_at] - pivots[shell_at] * solved_v[0])
    solved_w.insert(0, sweep_w[shell_at] - pivots[shell_at] * solved_w[0])
    first_u, last_u = (solved_u[0], solved_u[-1])
    first_v, last_v = (solved_v[0], solved_v[-1])
    first_w, last_w = (solved_w[0], solved_w[-1])
    wide_rows = jnp.stack([first_u, last_u])[None]
    narrow_rows = jnp.stack([first_v, first_w, last_v, last_w])[None]
    wide_all, narrow_all = (
        lax.all_gather(wide_rows, "radial", axis=0, tiled=True),
        lax.all_gather(narrow_rows, "radial", axis=0, tiled=True),
    )
    chain_count = lax.axis_size("radial")
    alpha_now, beta_now = (wide_zero, narrow_zero)
    alphas, betas = ([], [])
    for member in range(chain_count):
        alphas.append(alpha_now)
        betas.append(beta_now)
        peer_first_u, peer_last_u = (wide_all[member, 0], wide_all[member, 1])
        peer_first_v, peer_first_w = (narrow_all[member, 0], narrow_all[member, 1])
        peer_last_v, peer_last_w = (narrow_all[member, 2], narrow_all[member, 3])
        shrink = 1.0 - peer_first_v * beta_now
        alpha_new = (
            peer_last_u
            - peer_last_u * peer_first_v * beta_now
            + peer_last_v * alpha_now
            + peer_last_v * peer_first_u * beta_now
        ) / shrink
        beta_new = (
            peer_last_w
            - peer_last_w * peer_first_v * beta_now
            + peer_last_v * peer_first_w * beta_now
        ) / shrink
        alpha_now, beta_now = (alpha_new, beta_new)
    next_first = wide_zero
    firsts = [None] * chain_count
    nexts = [None] * chain_count
    for member in range(chain_count - 1, -1, -1):
        nexts[member] = next_first
        peer_first_u = wide_all[member, 0]
        peer_first_v, peer_first_w = (narrow_all[member, 0], narrow_all[member, 1])
        next_first = (peer_first_u + peer_first_v * alphas[member] + peer_first_w * next_first) / (
            1.0 - peer_first_v * betas[member]
        )
        firsts[member] = next_first
    alpha_prev = lax.dynamic_index_in_dim(jnp.stack(alphas), radial_at, 0, keepdims=False)
    beta_prev = lax.dynamic_index_in_dim(jnp.stack(betas), radial_at, 0, keepdims=False)
    own_first = lax.dynamic_index_in_dim(jnp.stack(firsts), radial_at, 0, keepdims=False)
    next_first = lax.dynamic_index_in_dim(jnp.stack(nexts), radial_at, 0, keepdims=False)
    prev_last = alpha_prev + beta_prev * own_first
    outputs = []
    for shell_at in range(shell_count):
        outputs.append(
            solved_u[shell_at] + prev_last * solved_v[shell_at] + next_first * solved_w[shell_at]
        )
    return jnp.stack(outputs, axis=2)


def solution(mesh):
    placed = (P("mode", None, "radial", None, None), P("mode", None, "radial"), P(), P(), P())
    return jax.shard_map(
        body,
        mesh=mesh,
        in_specs=placed,
        out_specs=P("mode", None, "radial", None, None),
        check_vma=False,
    )
```

profile of v0, /device:TPU:0, one launch (start us, length us, event | category | flops | bytes accessed | tf_op | source)
XLA Modules:
  0.0 39.1 jit_solution(3791041279454272241)
XLA Ops:
  0.0 0.0 copy-start
  0.0 0.0 copy-start.4
  0.0 0.0 copy-start.1
  0.0 0.7 %copy-done.4 = s32[64]{0:T(128)S(1)} copy-done((s32[64]{0:T(128)S(1)}, s32[64]{0:T(128)}, u32[]{:S(2)}) %copy-start.4) | copy-done | bytes 280
  0.7 0.1 broadcast_subtract_fusion.2
  0.8 0.1 fusion.76
  0.9 0.0 copy-done.1
  1.0 0.0 copy-done
  1.0 0.2 convolution_bitcast_fusion
  1.2 0.1 rev.6
  1.4 0.4 copy.85
  1.8 1.0 %reshape.1034 = bf16[32,2,192]{2,1,0:T(2,128)(2,1)} reshape(bf16[256,3,2,8]{3,2,1,0:T(2,128)(2,1)S(1)} %bitcast.154) | data formatting | bytes 49152
  2.8 7.3 %all-to-all-start = ((bf16[32,2,192]{2,1,0:T(2,128)(2,1)}), bf16[32,2,192]{2,1,0:T(2,128)(2,1)S(1)}, u32[]{:S(2)}, u32[]{:S(2)}) async-start(bf16[32,2,192]{2,1,0:T(2,128)(2,1)} %reshape.1034), calls=%async_computation | async-start | bytes 65536 | tf_op jit(solution)/shard_map/all_to_all | solution.py:77
  10.1 0.7 %collective-permute-start = (bf16[2,3,1,2,129]{4,1,3,0,2:T(4,128)(2,1)S(1)}, bf16[2,3,1,2,129]{4,1,3,0,2:T(4,128)(2,1)S(1)}, u32[]{:S(2)}, u32[]{:S(2)}) collective-permute-start(bf16[2,3,1,2,129]{4,1,3,0,2:T(4,128)(2,1)S(1)} %get-tuple-element.20), channel_id=1, source_target_pairs={} | collective-permute-start | bytes 9296 | tf_op jit(solution)/shard_map/ppermute | solution.py:20
  10.8 0.7 %collective-permute-start.1 = (bf16[2,3,1,2,129]{4,1,3,0,2:T(4,128)(2,1)S(1)}, bf16[2,3,1,2,129]{4,1,3,0,2:T(4,128)(2,1)S(1)}, u32[]{:S(2)}, u32[]{:S(2)}) collective-permute-start(bf16[2,3,1,2,129]{4,1,3,0,2:T(4,128)(2,1)S(1)} %get-tuple-element.21), channel_id=1, source_target_pairs={} | collective-permute-start | bytes 9296 | tf_op jit(solution)/shard_map/ppermute | solution.py:21
  11.4 0.1 broadcast_in_dim.114
  11.6 0.0 copy-start.2
  11.6 0.1 broadcast_multiply_fusion.4
  11.7 0.6 %copy-done.2 = f32[3]{0:T(128)S(1)} copy-done((f32[3]{0:T(128)S(1)}, f32[3]{0:T(128)}, u32[]{:S(2)}) %copy-start.2) | copy-done | bytes 36
  12.2 0.1 multiply_subtract_fusion.2
  12.3 0.1 broadcast_multiply_fusion.3
  12.5 0.1 broadcast_select_fusion
  12.6 0.1 reshape.1025
  12.8 0.1 broadcast_in_dim.120
  12.9 0.1 broadcast_in_dim.121
  13.0 4.3 %all-to-all-done = bf16[32,2,192]{2,1,0:T(2,128)(2,1)S(1)} async-done(((bf16[32,2,192]{2,1,0:T(2,128)(2,1)}), bf16[32,2,192]{2,1,0:T(2,128)(2,1)S(1)}, u32[]{:S(2)}, u32[]{:S(2)}) %all-to-all-start) | async-done | bytes 24608 | tf_op jit(solution)/shard_map/all_to_all | solution.py:77
  17.3 0.3 reshape.1035
  17.7 0.3 copy.86
  17.9 0.5 %reshape.1029 = f32[32,8,2,3,8]{1,0,4,3,2:T(8,128)S(1)} reshape(bf16[256,2,3,8]{0,3,2,1:T(8,128)(2,1)S(1)} %copy.86) | data formatting | bytes 73728 | tf_op jit(solution)/shard_map/convert_element_type | solution.py:87
  18.4 0.9 %copy.87 = f32[8,2,3,32,8]{4,3,0,2,1:T(8,128)S(1)} copy(f32[8,2,3,32,8]{0,3,4,2,1:T(8,128)S(1)} %bitcast.152) | data formatting | bytes 98304 | tf_op jit(solution)/shard_map/convert_element_type | solution.py:87
  19.3 0.4 %reshape.1028 = f32[8,2,3,256]{3,0,2,1:T(8,128)S(1)} reshape(f32[8,2,3,32,8]{4,3,0,2,1:T(8,128)S(1)} %copy.87) | data formatting | bytes 98304 | tf_op jit(solution)/shard_map/convert_element_type | solution.py:87
  19.7 2.0 %fusion.6 = f32[8,2,3,384]{3,0,2,1:T(8,128)S(1)} fusion(s32[256]{0:T(256)S(1)} %reshape.1025, pred[256]{0:T(512)(128)(4,1)S(1)} %broadcast_in_dim.121, f32[8,2,3,256]{3,0,2,1:T(8,128)S(1)} %reshape.1028, f32[256]{0:T(256)S(1)} %compare_select_fusion.5), kind=kOutput, calls=%fused_computation.10 | convolution fusion | flops 57716736 | bytes 125184 | tf_op jit(solution)/shard_map/dot_general | solution.py:94
  21.8 2.1 %fusion.3 = bf16[48,256]{1,0:T(8,128)(2,1)S(1)} fusion(f32[48,384]{1,0:T(8,128)S(1)} %reshape.1026, s32[256]{0:T(256)S(1)} %reshape.1025, pred[256]{0:T(512)(128)(4,1)S(1)} %broadcast_in_dim.121), kind=kOutput, calls=%fused_computation.6 | convolution fusion | flops 57729024 | bytes 99584 | tf_op jit(solution)/shard_map/dot_general | solution.py:104
  24.0 0.4 copy.89
  24.4 1.0 %reshape.1036 = bf16[32,2,192]{2,1,0:T(2,128)(2,1)} reshape(bf16[256,3,2,8]{3,2,1,0:T(2,128)(2,1)S(1)} %bitcast.157) | data formatting | bytes 49152
  25.4 2.5 %all-to-all-start.1 = ((bf16[32,2,192]{2,1,0:T(2,128)(2,1)}), bf16[32,2,192]{2,1,0:T(2,128)(2,1)S(1)}, u32[]{:S(2)}, u32[]{:S(2)}) async-start(bf16[32,2,192]{2,1,0:T(2,128)(2,1)} %reshape.1036), calls=%async_computation.1 | async-start | bytes 65536 | tf_op jit(solution)/shard_map/all_to_all | solution.py:111
  27.9 0.0 collective-permute-done
  27.9 0.0 collective-permute-done.1
  28.0 7.2 %all-to-all-done.1 = bf16[32,2,192]{2,1,0:T(2,128)(2,1)S(1)} async-done(((bf16[32,2,192]{2,1,0:T(2,128)(2,1)}), bf16[32,2,192]{2,1,0:T(2,128)(2,1)S(1)}, u32[]{:S(2)}, u32[]{:S(2)}) %all-to-all-start.1) | async-done | bytes 24608 | tf_op jit(solution)/shard_map/all_to_all | solution.py:111
  35.2 0.3 reshape.1037
  35.5 0.6 %copy.108 = bf16[8,2,3,32,8]{4,3,0,2,1:T(8,128)(2,1)S(1)} copy(bf16[8,2,3,32,8]{0,1,2,4,3:T(2,128)(2,1)S(1)} %bitcast.156) | data formatting | bytes 49152 | tf_op jit(solution)/shard_map/all_to_all | solution.py:111
  36.1 0.3 copy.91
  36.4 0.2 slice.78
  36.6 0.3 copy.94
  36.9 0.2 slice.80
  37.1 0.1 rev.7
  37.2 0.2 fusion.23
  37.4 0.2 fusion.2
  37.6 0.0 copy-start.3
  37.6 0.6 %copy-done.3 = f32[3]{0:T(128)S(1)} copy-done((f32[3]{0:T(128)S(1)}, f32[3]{0:T(128)}, u32[]{:S(2)}) %copy-start.3) | copy-done | bytes 36
  38.3 0.1 multiply_subtract_fusion
  38.4 0.1 add_add_fusion.1
  38.5 0.6 %copy.99 = f32[2,3,2,2,129]{4,3,2,1,0:T(2,128)} copy(f32[2,3,2,2,129]{4,1,3,0,2:T(4,128)S(1)} %pad_maximum_fusion.1) | data formatting | bytes 24768 | tf_op jit(solution)/shard_map/stack | solution.py:233
  (27 shorter events, 0.4 us)
Async XLA Ops:
  0.0 1.0 %copy-start = (bf16[2,129,128]{2,0,1:T(2,128)(2,1)S(1)}, bf16[2,129,128]{2,0,1:T(2,128)(2,1)}, u32[]{:S(2)}) copy-start(bf16[2,129,128]{2,0,1:T(2,128)(2,1)} %param.6) | copy-start | bytes 198148
  0.0 0.7 %copy-start.4 = (s32[64]{0:T(128)S(1)}, s32[64]{0:T(128)}, u32[]{:S(2)}) copy-start(s32[64]{0:T(128)} %param.7) | copy-start | bytes 772
  0.0 0.9 %copy-start.1 = (f32[2,3,2,2,129]{4,3,2,1,0:T(2,128)S(1)}, f32[2,3,2,2,129]{4,3,2,1,0:T(2,128)}, u32[]{:S(2)}) copy-start(f32[2,3,2,2,129]{4,3,2,1,0:T(2,128)} %param.5) | copy-start | bytes 37156
  2.8 14.6 %all-to-all-start = ((bf16[32,2,192]{2,1,0:T(2,128)(2,1)}), bf16[32,2,192]{2,1,0:T(2,128)(2,1)S(1)}, u32[]{:S(2)}, u32[]{:S(2)}) async-start(bf16[32,2,192]{2,1,0:T(2,128)(2,1)} %reshape.1034), calls=%async_computation | async-start | bytes 65536 | tf_op jit(solution)/shard_map/all_to_all | solution.py:77
  10.1 17.8 %collective-permute-start = (bf16[2,3,1,2,129]{4,1,3,0,2:T(4,128)(2,1)S(1)}, bf16[2,3,1,2,129]{4,1,3,0,2:T(4,128)(2,1)S(1)}, u32[]{:S(2)}, u32[]{:S(2)}) collective-permute-start(bf16[2,3,1,2,129]{4,1,3,0,2:T(4,128)(2,1)S(1)} %get-tuple-element.20), channel_id=1, source_target_pairs={} | collective-permute-start | bytes 9296 | tf_op jit(solution)/shard_map/ppermute | solution.py:20
  10.8 17.2 %collective-permute-start.1 = (bf16[2,3,1,2,129]{4,1,3,0,2:T(4,128)(2,1)S(1)}, bf16[2,3,1,2,129]{4,1,3,0,2:T(4,128)(2,1)S(1)}, u32[]{:S(2)}, u32[]{:S(2)}) collective-permute-start(bf16[2,3,1,2,129]{4,1,3,0,2:T(4,128)(2,1)S(1)} %get-tuple-element.21), channel_id=1, source_target_pairs={} | collective-permute-start | bytes 9296 | tf_op jit(solution)/shard_map/ppermute | solution.py:21
  11.6 0.7 %copy-start.2 = (f32[3]{0:T(128)S(1)}, f32[3]{0:T(128)}, u32[]{:S(2)}) copy-start(f32[3]{0:T(128)} %param.8) | copy-start | bytes 40
  25.4 9.8 %all-to-all-start.1 = ((bf16[32,2,192]{2,1,0:T(2,128)(2,1)}), bf16[32,2,192]{2,1,0:T(2,128)(2,1)S(1)}, u32[]{:S(2)}, u32[]{:S(2)}) async-start(bf16[32,2,192]{2,1,0:T(2,128)(2,1)} %reshape.1036), calls=%async_computation.1 | async-start | bytes 65536 | tf_op jit(solution)/shard_map/all_to_all | solution.py:111
  37.6 0.7 %copy-start.3 = (f32[3]{0:T(128)S(1)}, f32[3]{0:T(128)}, u32[]{:S(2)}) copy-start(f32[3]{0:T(128)} %param.9) | copy-start | bytes 40
where the time goes:
time: 39.4 us; the launch traced here: 39.1 us
  waiting for transfers between devices  11.5 us (29%)
  starting transfers between devices  11.2 us (28%)
  local copies, waits for them, and re-layouts  10.3 us (26%)
  matrix products  4.71 us (12%)
  other arithmetic  1.02 us (3%)
  between operations  0.42 us (1%)
    all_to_all x1, starting transfers between devices, body(): lax.all_to_all(joined.reshape(lat_total, shell_count, coeffs.shape[1], 4...  7.33 us
    all_to_all x1, waiting for transfers between devices, body(): lax.all_to_all(answers.reshape(lat_dev, item_count, field_count, column_c...  7.2 us
    unnamed x15, local copies, waits for them, and re-layouts  4.52 us
    all_to_all x1, waiting for transfers between devices, body(): lax.all_to_all(joined.reshape(lat_total, shell_count, coeffs.shape[1], 4...  4.32 us
    all_to_all x1, starting transfers between devices, body(): lax.all_to_all(answers.reshape(lat_dev, item_count, field_count, column_c...  2.52 us
    dot_general x1, matrix products, body(): lax.dot_general(products.reshape(row_total, block_size), wave_table, (((1...  2.15 us
    dot_general x1, matrix products, body(): values = jnp.dot(weighted, wave_table, precision=lax.Precision.HIGHEST)  2.03 us
    convert_element_type x3, local copies, waits for them, and re-layouts, body(): pieces.reshape(row_total, column_count).astype(jnp.float32)  1.73 us
  transfers between devices with their start and end apart: 4, of which 2 were waited for; matrix products, arithmetic and copies ran while one was open for 23% of the time, Pallas kernels for 0%

commit v1 on v0

v1 whole, which is shorter than its diff:
```python
import functools
import math

import jax
import jax.numpy as jnp
from jax import lax
from jax.experimental import pallas as pl
from jax.experimental.pallas import tpu as pltpu
from jax.sharding import PartitionSpec as P

inner_radius = 0.538
shell_step = 1.0 / 2048.0
LANES = 128
GRANT = pltpu.CompilerParams(vmem_limit_bytes=16 * 1024 * 1024)
NT = (((1,), (1,)), ((), ()))


def with_halo(shard, axis, dim, width):
    count, length = (lax.axis_size(axis), shard.shape[dim])
    up = [(i, (i + 1) % count) for i in range(count - 1)]
    down = [(j, i) for i, j in up]
    last = lax.slice_in_dim(shard, length - width, length, axis=dim)
    first = lax.slice_in_dim(shard, 0, width, axis=dim)
    before = lax.ppermute(last, axis, up)
    after = lax.ppermute(first, axis, down)
    return jnp.concatenate([before, shard, after], axis=dim)


def row_factors(lower, shape, orders_total):
    row = lax.broadcasted_iota(jnp.int32, shape, len(shape) - 1)
    in_lower = row < orders_total - lower
    odd_lower = lax.rem(row, 2) == 1
    odd_upper = lax.rem(row + orders_total - lower, 2) == 1
    members = (in_lower, jnp.logical_not(in_lower))
    signs = (jnp.where(odd_lower, -1.0, 1.0), jnp.where(odd_upper, -1.0, 1.0))
    return members, signs


def state_rows(state_ref, pair, part, fields):
    shells = state_ref.shape[2]
    rows = [state_ref[pair, f, s, part : part + 1, :] for f in fields for s in range(shells)]
    return jnp.concatenate(rows, axis=0)


def fill_waves(low_row, orders_total, high_ref, rest_ref, step):
    columns, lon_total = high_ref.shape
    width = lon_total // 3
    lon = lax.broadcasted_iota(jnp.int32, (step, width), 1).astype(jnp.float32)
    pair_lane = lax.broadcasted_iota(jnp.int32, (step, low_row.shape[1]), 1)
    third = math.sqrt(0.75)

    def fill(base):
        column = base + lax.broadcasted_iota(jnp.int32, (step, 1), 0)
        hit = pair_lane == column // 4
        lower = jnp.sum(jnp.where(hit, low_row, 0.0), axis=1, keepdims=True)
        is_lower = (column // 2) % 2 == 0
        is_cosine = column % 2 == 0
        order = jnp.where(is_lower, lower, orders_total - 1 - lower)
        turns = order * lon
        quad = jnp.floor(turns * (4.0 / lon_total) + 0.5)
        angle = (turns - quad * (lon_total / 4)) * (2.0 * math.pi / lon_total)
        square = angle * angle
        cosine = 1.0 + square * (
            -0.5 + square * (1.0 / 24 + square * (-1.0 / 720 + square * (1.0 / 40320)))
        )
        sine = 1.0 / 120 + square * (-1.0 / 5040 + square * (1.0 / 362880))
        sine = angle * (1.0 + square * (-1.0 / 6 + square * sine))
        quad = quad.astype(jnp.int32)
        swap = (quad & 1) == 1
        cosine, sine = (jnp.where(swap, sine, cosine), jnp.where(swap, cosine, sine))
        cosine = jnp.where(((quad + 1) & 2) == 2, -cosine, cosine)
        sine = jnp.where((quad & 2) == 2, -sine, sine)
        for at in range(3):
            turn = at * order
            turn = turn - 3.0 * jnp.floor((turn + 0.5) * (1.0 / 3.0))
            cos_at = jnp.where(turn == 0.0, 1.0, -0.5)
            sin_at = jnp.where(turn == 0.0, 0.0, jnp.where(turn == 1.0, third, -third))
            by_cosine = jnp.where(is_cosine, cos_at, -sin_at)
            by_sine = jnp.where(is_cosine, -sin_at, -cos_at)
            value = cosine * by_cosine + sine * by_sine
            high = value.astype(jnp.bfloat16)
            high_ref[pl.ds(base, step), at * width : (at + 1) * width] = high
            rest_ref[pl.ds(base, step), at * width : (at + 1) * width] = (
                value - high.astype(jnp.float32)
            ).astype(jnp.bfloat16)

    if columns <= 256:
        for base in range(0, columns, step):
            fill(base)
    else:

        @pl.loop(0, columns // step)
        def _(at):
            fill(pl.multiple_of(at * step, step))


def synthesis_kernel(
    dims, low_ref, low_row_ref, state_ref, table_ref, out_ref, high_ref, rest_ref, spread_ref
):
    pairs_dev, block, mode_count, orders_total = dims
    fields = state_ref.shape[1]
    rows_total = state_ref.shape[-1]
    chunk_rows = out_ref.shape[0] // mode_count
    group = lax.axis_index("mode") * pairs_dev
    pieces = []
    for pair in range(pairs_dev):
        lower = low_ref[group + pair]
        members, signs = row_factors(lower, (1, rows_total), orders_total)
        coeffs = [state_rows(state_ref, pair, part, (*range(fields), 0)) for part in range(2)]
        left = []
        for k in range(2):
            order = lower if k == 0 else orders_total - 1 - lower
            weight = jnp.where(order == 0, 1.0, 2.0)
            member = jnp.where(members[k], weight, 0.0)
            for part in range(2):
                left.append(coeffs[part] * member)
                left.append(coeffs[part] * (member * signs[k]))
        left = jnp.concatenate(left, axis=0).astype(jnp.bfloat16)
        pieces.append(jnp.dot(left, table_ref[pair], preferred_element_type=jnp.float32))
    fourier = jnp.concatenate(pieces, axis=0).astype(jnp.bfloat16).astype(jnp.float32)
    turned = fourier.T
    lane_block = lax.broadcasted_iota(jnp.int32, (mode_count, LANES), 1) // block
    count = turned.shape[0] // mode_count
    for row in range(chunk_rows):
        merged = jnp.zeros((mode_count, LANES), jnp.float32)
        for i in range(count):
            part = turned[i * mode_count : (i + 1) * mode_count]
            moved = pltpu.roll(part, (block * (i - row)) % LANES, 1)
            merged = jnp.where(lane_block == i, moved, merged)
        spread_ref[:, row, :] = merged
    out_ref[...] = spread_ref[...].reshape(out_ref.shape).astype(jnp.bfloat16)
    fill_waves(low_row_ref[...].astype(jnp.float32), orders_total, high_ref, rest_ref, 32)


def product_kernel(dims, sent_ref, high_ref, rest_ref, out_ref):
    used, shells, scale = dims
    turned = sent_ref[...].astype(jnp.float32).T[:used].astype(jnp.bfloat16)
    grid = jnp.dot(turned, high_ref[...], preferred_element_type=jnp.float32)
    grid = grid + jnp.dot(turned, rest_ref[...], preferred_element_type=jnp.float32)
    products = grid * pltpu.roll(grid, used - shells, 0)
    high = products.astype(jnp.bfloat16)
    rest = (products - high.astype(jnp.float32)).astype(jnp.bfloat16)
    both = lax.dot_general(
        high_ref[...], jnp.concatenate([high, rest], axis=0), NT, preferred_element_type=jnp.float32
    )
    totals = lax.dot_general(rest_ref[...], high, NT, preferred_element_type=jnp.float32)
    totals = totals + both[:, :used] + both[:, used:]
    answers = (totals * scale).astype(jnp.bfloat16)
    out_ref[...] = jnp.concatenate(
        [answers, jnp.zeros((answers.shape[0], LANES - used), jnp.bfloat16)], axis=1
    )


def analysis_sums(dims, low_ref, sent_ref, table_ref, spread_ref, emit):
    pairs_dev, block, count, mode_count, orders_total = dims
    rows_total = table_ref.shape[1]
    chunk_rows = sent_ref.shape[0] // mode_count
    group = lax.axis_index("mode") * pairs_dev
    spread_ref[...] = sent_ref[...].astype(jnp.float32).reshape(spread_ref.shape)
    lane_block = lax.broadcasted_iota(jnp.int32, (mode_count, LANES), 1) // block
    parts = [jnp.zeros((mode_count, LANES), jnp.float32) for _ in range(count)]
    for row in range(chunk_rows):
        piece = spread_ref[:, row, :]
        for i in range(count):
            moved = pltpu.roll(piece, (block * (row - i)) % LANES, 1)
            parts[i] = jnp.where(lane_block == row, moved, parts[i])
    returned = jnp.concatenate(parts, axis=0).T.astype(jnp.bfloat16)
    per_pair = returned.shape[0] // pairs_dev
    half = block // 2
    for pair in range(pairs_dev):
        lower = low_ref[group + pair]
        members, signs = row_factors(lower, (1, rows_total), orders_total)
        sums = lax.dot_general(
            returned[pair * per_pair : (pair + 1) * per_pair],
            table_ref[pair],
            NT,
            preferred_element_type=jnp.float32,
        )
        for part in range(2):
            total = jnp.zeros((half, rows_total), jnp.float32)
            for k in range(2):
                at = (k * 2 + part) * block
                north = sums[at : at + half]
                south = sums[at + half : at + block]
                total = jnp.where(members[k], north + signs[k] * south, total)
            emit(pair, part, lower, total)


def analysis_kernel(dims, low_ref, sent_ref, table_ref, out_ref, spread_ref):
    def emit(pair, part, lower, total):
        out_ref[pair, part] = total

    analysis_sums(dims, low_ref, sent_ref, table_ref, spread_ref, emit)


def step_kernel(
    dims, low_ref, rate_ref, coupling_ref, sent_ref, table_ref, state_ref, out_ref, spread_ref
):
    orders_total = dims[-1]
    rows_total = table_ref.shape[1]
    half = dims[1] // 2
    fields = (0, 2, 1, 0)
    at = lax.broadcasted_iota(jnp.int32, (half, 1), 0)
    upper = at % 2 == 1
    by_field = [at // 2 == 1, at // 2 == 2]

    def column(ref):
        first = jnp.full((half, 1), ref[0], jnp.float32)
        return jnp.where(by_field[0], ref[2], jnp.where(by_field[1], ref[1], first))

    def other(value):
        return jnp.where(upper, pltpu.roll(value, 1, 0), pltpu.roll(value, half - 1, 0))

    rate = column(rate_ref)
    strength = column(coupling_ref)
    radius = inner_radius + (jnp.where(upper, 1.0, 0.0) + 0.5) * shell_step
    inverse = (shell_step * shell_step) / (radius * radius)
    row = lax.broadcasted_iota(jnp.int32, (1, rows_total), 1)
    cache = {}

    def emit(pair, part, lower, total):
        if pair not in cache:
            degree = jnp.where(row < orders_total - lower, lower + row, row - 1).astype(jnp.float32)
            damping = (degree * (degree + 1.0)) * inverse
            diagonal = 1.0 + rate * (2.0 + damping)
            crossed = other(diagonal)
            factor = 1.0 / (diagonal * crossed - rate * rate)
            cache[pair] = (damping, crossed * factor, rate * factor)
        damping, own, across = cache[pair]
        state = state_rows(state_ref, pair, part, fields)
        laplace = other(state) - 2.0 * state - damping * state
        drive = state + rate * (laplace + strength * total)
        updated = own * drive + across * other(drive)
        for k, f in enumerate(fields[:3]):
            for s in range(2):
                out_ref[pair, f, s, part : part + 1, :] = updated[2 * k + s : 2 * k + s + 1]

    analysis_sums(dims, low_ref, sent_ref, table_ref, spread_ref, emit)


def vmem(count):
    return [pl.BlockSpec(memory_space=pltpu.VMEM)] * count


def body(spectral_state, synthesis_table, low_orders, diffusion, coupling):
    radial_count = lax.axis_size("radial")
    if radial_count > 1:
        synthesis_table = lax.all_gather(synthesis_table, "radial", axis=2, tiled=True)
    pairs_dev, field_count, shell_count, part_count, rows_total = spectral_state.shape
    half_lat = synthesis_table.shape[2]
    lat_total = 2 * half_lat
    orders_total = rows_total - 1
    lon_total = 3 * orders_total
    mode_count = lax.axis_size("mode")
    chunk_rows = pairs_dev * 2 * part_count
    column_count = chunk_rows * mode_count
    count = half_lat // mode_count
    half = (field_count + 1) * shell_count
    block = 2 * half
    used = count * block
    assert half == 8 and chunk_rows * block == LANES and used <= LANES // 2 and part_count == 2
    scale = 2.0 * math.sqrt(orders_total * rows_total / (lat_total * lon_total))
    low_orders = low_orders.astype(jnp.int32)
    smem = pl.BlockSpec(memory_space=pltpu.SMEM)
    spread = pltpu.VMEM((mode_count, chunk_rows, LANES), jnp.float32)
    sent = jax.ShapeDtypeStruct((column_count, LANES), jnp.bfloat16)
    table_shape = jax.ShapeDtypeStruct((column_count, lon_total), jnp.bfloat16)
    chunks, wave_high, wave_rest = pl.pallas_call(
        functools.partial(synthesis_kernel, (pairs_dev, block, mode_count, orders_total)),
        out_shape=[sent, table_shape, table_shape],
        in_specs=[smem] + vmem(3),
        out_specs=vmem(3),
        scratch_shapes=[spread],
        compiler_params=GRANT,
        name="synthesis",
    )(low_orders, low_orders[None, :], spectral_state, synthesis_table)
    pieces = lax.all_to_all(chunks, "mode", split_axis=0, concat_axis=0, tiled=True)
    answers = pl.pallas_call(
        functools.partial(product_kernel, (used, shell_count, scale)),
        out_shape=sent,
        in_specs=vmem(3),
        out_specs=pl.BlockSpec(memory_space=pltpu.VMEM),
        compiler_params=GRANT,
        name="products",
    )(pieces, wave_high, wave_rest)
    returned = lax.all_to_all(answers, "mode", split_axis=0, concat_axis=0, tiled=True)
    dims = (pairs_dev, block, count, mode_count, orders_total)
    if radial_count == 1 and shell_count == 2:
        return pl.pallas_call(
            functools.partial(step_kernel, dims),
            out_shape=jax.ShapeDtypeStruct(spectral_state.shape, jnp.float32),
            in_specs=[smem] * 3 + vmem(3),
            out_specs=pl.BlockSpec(memory_space=pltpu.VMEM),
            scratch_shapes=[spread],
            compiler_params=GRANT,
            name="step",
        )(low_orders, diffusion, coupling, returned, synthesis_table, spectral_state)
    nonlinear = pl.pallas_call(
        functools.partial(analysis_kernel, dims),
        out_shape=jax.ShapeDtypeStruct((pairs_dev, part_count, half, rows_total), jnp.float32),
        in_specs=[smem] + vmem(2),
        out_specs=pl.BlockSpec(memory_space=pltpu.VMEM),
        scratch_shapes=[spread],
        compiler_params=GRANT,
        name="analysis",
    )(low_orders, returned, synthesis_table)
    nonlinear = nonlinear.reshape(pairs_dev, part_count, field_count + 1, shell_count, rows_total)
    nonlinear = jnp.stack([nonlinear[:, :, 0], nonlinear[:, :, 2], nonlinear[:, :, 1]], axis=1)
    nonlinear = nonlinear.transpose(0, 1, 3, 2, 4)
    return solve(spectral_state, nonlinear, low_orders, diffusion, coupling)


def solve(spectral_state, nonlinear, low_orders, diffusion, coupling):
    pairs_dev, field_count, shell_count, part_count, rows_total = spectral_state.shape
    orders_total = rows_total - 1
    radial_count = lax.axis_size("radial")
    own = lax.dynamic_slice_in_dim(low_orders, lax.axis_index("mode") * pairs_dev, pairs_dev)
    row_index = lax.iota(jnp.int32, rows_total)[None, :]
    lower_col = own[:, None]
    degree = jnp.where(row_index < orders_total - lower_col, lower_col + row_index, row_index - 1)
    radial_at = lax.axis_index("radial")
    rate_col = diffusion.reshape(1, field_count, 1, 1)
    strength = coupling.reshape(1, field_count, 1, 1)
    degree_term = degree.astype(jnp.float32)
    degree_term = (degree_term * (degree_term + 1.0))[:, None, None, :] * (shell_step * shell_step)
    if radial_count > 1:
        with_edges = with_halo(spectral_state, "radial", 2, 1)
    else:
        with_edges = jnp.pad(spectral_state, ((0, 0), (0, 0), (1, 1), (0, 0), (0, 0)))
    diagonals = []
    drives = []
    for shell_at in range(shell_count):
        radius = (
            inner_radius
            + ((radial_at * shell_count + shell_at).astype(jnp.float32) + 0.5) * shell_step
        )
        damping = degree_term / (radius * radius)
        middle = with_edges[:, :, shell_at + 1]
        laplace = (
            with_edges[:, :, shell_at + 2]
            - 2.0 * middle
            + with_edges[:, :, shell_at]
            - damping * middle
        )
        drives.append(middle + rate_col * (laplace + strength * nonlinear[:, :, shell_at]))
        diagonals.append(1.0 + rate_col * (2.0 + damping))
    narrow_zero = jnp.zeros(diagonals[0].shape, jnp.float32)
    wide_zero = jnp.zeros(drives[0].shape, jnp.float32)
    pivot_prev = narrow_zero
    carry_u, carry_v, carry_w = (wide_zero, narrow_zero, narrow_zero)
    pivots, sweep_u, sweep_v, sweep_w = ([], [], [], [])
    for shell_at in range(shell_count):
        denom_at = diagonals[shell_at] + rate_col * pivot_prev
        pivot_prev = -rate_col / denom_at
        first_drive = rate_col if shell_at == 0 else 0.0
        last_drive = rate_col if shell_at == shell_count - 1 else 0.0
        carry_u = (drives[shell_at] + rate_col * carry_u) / denom_at
        carry_v = (first_drive + rate_col * carry_v) / denom_at
        carry_w = (last_drive + rate_col * carry_w) / denom_at
        pivots.append(pivot_prev)
        sweep_u.append(carry_u)
        sweep_v.append(carry_v)
        sweep_w.append(carry_w)
    solved_u, solved_v, solved_w = ([sweep_u[-1]], [sweep_v[-1]], [sweep_w[-1]])
    for shell_at in range(shell_count - 2, -1, -1):
        solved_u.insert(0, sweep_u[shell_at] - pivots[shell_at] * solved_u[0])
        solved_v.insert(0, sweep_v[shell_at] - pivots[shell_at] * solved_v[0])
        solved_w.insert(0, sweep_w[shell_at] - pivots[shell_at] * solved_w[0])
    if radial_count == 1:
        return jnp.stack(solved_u, axis=2)
    first_u, last_u = (solved_u[0], solved_u[-1])
    first_v, last_v = (solved_v[0], solved_v[-1])
    first_w, last_w = (solved_w[0], solved_w[-1])
    wide_rows = jnp.stack([first_u, last_u])[None]
    narrow_rows = jnp.stack([first_v, first_w, last_v, last_w])[None]
    wide_all, narrow_all = (
        lax.all_gather(wide_rows, "radial", axis=0, tiled=True),
        lax.all_gather(narrow_rows, "radial", axis=0, tiled=True),
    )
    chain_count = lax.axis_size("radial")
    alpha_now, beta_now = (wide_zero, narrow_zero)
    alphas, betas = ([], [])
    for member in range(chain_count):
        alphas.append(alpha_now)
        betas.append(beta_now)
        peer_first_u, peer_last_u = (wide_all[member, 0], wide_all[member, 1])
        peer_first_v, peer_first_w = (narrow_all[member, 0], narrow_all[member, 1])
        peer_last_v, peer_last_w = (narrow_all[member, 2], narrow_all[member, 3])
        shrink = 1.0 - peer_first_v * beta_now
        alpha_new = (
            peer_last_u
            - peer_last_u * peer_first_v * beta_now
            + peer_last_v * alpha_now
            + peer_last_v * peer_first_u * beta_now
        ) / shrink
        beta_new = (
            peer_last_w
            - peer_last_w * peer_first_v * beta_now
            + peer_last_v * peer_first_w * beta_now
        ) / shrink
        alpha_now, beta_now = (alpha_new, beta_new)
    next_first = wide_zero
    firsts = [None] * chain_count
    nexts = [None] * chain_count
    for member in range(chain_count - 1, -1, -1):
        nexts[member] = next_first
        peer_first_u = wide_all[member, 0]
        peer_first_v, peer_first_w = (narrow_all[member, 0], narrow_all[member, 1])
        next_first = (peer_first_u + peer_first_v * alphas[member] + peer_first_w * next_first) / (
            1.0 - peer_first_v * betas[member]
        )
        firsts[member] = next_first
    alpha_prev = lax.dynamic_index_in_dim(jnp.stack(alphas), radial_at, 0, keepdims=False)
    beta_prev = lax.dynamic_index_in_dim(jnp.stack(betas), radial_at, 0, keepdims=False)
    own_first = lax.dynamic_index_in_dim(jnp.stack(firsts), radial_at, 0, keepdims=False)
    next_first = lax.dynamic_index_in_dim(jnp.stack(nexts), radial_at, 0, keepdims=False)
    prev_last = alpha_prev + beta_prev * own_first
    outputs = []
    for shell_at in range(shell_count):
        outputs.append(
            solved_u[shell_at] + prev_last * solved_v[shell_at] + next_first * solved_w[shell_at]
        )
    return jnp.stack(outputs, axis=2)


def solution(mesh):
    placed = (P("mode", None, "radial", None, None), P("mode", None, "radial"), P(), P(), P())
    return jax.shard_map(
        body,
        mesh=mesh,
        in_specs=placed,
        out_specs=P("mode", None, "radial", None, None),
        check_vma=False,
    )
```

time: 39.4 us -> 29.6 us (0.75)
  blocking collectives: 0 us -> 23.6 us
  waiting for transfers between devices: 11.5 us -> 0 us
  starting transfers between devices: 11.2 us -> 0 us
  local copies, waits for them, and re-layouts: 10.3 us -> 2.21 us
  matrix products: 4.71 us -> 0 us
  Pallas kernels: 0 us -> 3.45 us
  other arithmetic: 1.02 us -> 0 us
    all_to_all x0 -> x2, blocking collectives: none -> 23.6 us  [the longest x1 14.5 us: body(): lax.all_to_all(chunks, 'mode', split_axis=0, concat_axis=0, tiled=True)]
    all_to_all x2 -> x0, waiting for transfers between devices: 11.5 us -> none  [the longest x1 7.2 us: body(): lax.all_to_all(answers.reshape(lat_dev, item_count, field_count, column_c...]
    all_to_all x2 -> x0, starting transfers between devices: 9.84 us -> none  [the longest x1 7.33 us: body(): lax.all_to_all(joined.reshape(lat_total, shell_count, coeffs.shape[1], 4...]
    dot_general x5 -> x0, matrix products: 4.71 us -> none  [the longest x1 2.15 us: body(): lax.dot_general(products.reshape(row_total, block_size), wave_table, (((1...]
    pallas_call x0 -> x3, Pallas kernels: none -> 3.45 us  [the longest x1 1.55 us: body(): pl.pallas_call(functools.partial(step_kernel, dims), out_shape=jax.ShapeD...]
    unnamed x15 -> x9, local copies, waits for them, and re-layouts: 4.52 us -> 2.21 us
    convert_element_type x3 -> x0, local copies, waits for them, and re-layouts: 1.73 us -> none  [body(): pieces.reshape(row_total, column_count).astype(jnp.float32)]
    ppermute x2 -> x0, starting transfers between devices: 1.31 us -> none  [the longest x1 0.65 us: with_halo(): after = lax.ppermute(first, axis, down)]
  transfers between devices with their start and end apart: 4 -> 0, of which waited for: 2 -> 0; matrix products, arithmetic and copies ran while one was open for 23% -> 0% of each run, Pallas kernels for 0% -> 0%
where the time goes in v1:
time: 29.6 us; the launch traced here: 29.3 us
  blocking collectives  23.6 us (80%)
  Pallas kernels  3.45 us (12%)
  local copies, waits for them, and re-layouts  2.21 us (7%)
    all_to_all x1, blocking collectives, body(): lax.all_to_all(chunks, 'mode', split_axis=0, concat_axis=0, tiled=True)  14.5 us
    all_to_all x1, blocking collectives, body(): lax.all_to_all(answers, 'mode', split_axis=0, concat_axis=0, tiled=True)  9.1 us
    unnamed x9, local copies, waits for them, and re-layouts  2.21 us
    pallas_call x1, Pallas kernels, body(): pl.pallas_call(functools.partial(step_kernel, dims), out_shape=jax.ShapeD...  1.55 us
    pallas_call x1, Pallas kernels, body(): pl.pallas_call(functools.partial(synthesis_kernel, (pairs_dev, block, mod...  1.33 us

profile of v1, /device:TPU:0, one launch (start us, length us, event | category | flops | bytes accessed | tf_op | source)
XLA Modules:
  0.0 29.3 jit_solution(5792255818968305398)
XLA Ops:
  0.0 0.0 copy-start
  0.0 0.9 %copy.6.table_ref = bf16[2,129,128]{2,1,0:T(8,128)(2,1)S(1)} copy(bf16[2,129,128]{2,0,1:T(2,128)(2,1)} %param.6) | data formatting | bytes 132096 | tf_op args[1]
  0.9 0.0 copy-start.1
  0.9 0.0 copy-done
  0.9 0.6 %copy-done.1 = s32[64]{0:T(128)S(1)} copy-done((s32[64]{0:T(128)S(1)}, s32[64]{0:T(128)}, u32[]{:S(2)}) %copy-start.1) | copy-done | bytes 280
  1.6 1.3 %synthesis.1 = (bf16[256,128]{1,0:T(8,128)(2,1)S(1)}, bf16[256,384]{1,0:T(8,128)(2,1)S(1)}, bf16[256,384]{1,0:T(8,128)(2,1)S(1)}) custom-call(s32[64]{0:T(128)S(1)} %copy-done.1, s32[1,64]{1,0:T(1,128)S(1)} %bitcast.9, f32[2,3,2,2,129]{4,3,2,1,0:T(2,128)S(1)} %copy-done, bf16[2,129,128]{2,1,0:T(8,128)(2,1)S(1)} %copy.6.table_ref), custom_call_target="tpu_custom_call" | custom-call | tf_op jit(solution)/shard_map/synthesis/pallas_call | solution.py:268
  2.9 14.5 %all_to_all.22 = bf16[32,8,128]{2,1,0:T(8,128)(2,1)S(1)} all-to-all(bf16[32,8,128]{2,1,0:T(8,128)(2,1)S(1)} %bitcast.8), channel_id=1, replica_groups=mesh['radial'=1,'mode'=32] {'mode'}, dimensions={0} | all-to-all | bytes 131072 | tf_op jit(solution)/shard_map/all_to_all | solution.py:277
  17.4 0.6 %products.1 = bf16[256,128]{1,0:T(8,128)(2,1)S(1)} custom-call(bf16[256,128]{1,0:T(8,128)(2,1)S(1)} %bitcast.6, bf16[256,384]{1,0:T(8,128)(2,1)S(1)} %get-tuple-element.9.high_ref, bf16[256,384]{1,0:T(8,128)(2,1)S(1)} %get-tuple-element.10.rest_ref), custom_call_target="tpu_custom_call" | custom-call | tf_op jit(solution)/shard_map/products/pallas_call | solution.py:278
  18.0 9.1 %all_to_all.23 = bf16[32,8,128]{2,1,0:T(8,128)(2,1)S(1)} all-to-all(bf16[32,8,128]{2,1,0:T(8,128)(2,1)S(1)} %bitcast.7), channel_id=1, replica_groups=mesh['radial'=1,'mode'=32] {'mode'}, dimensions={0} | all-to-all | bytes 131072 | tf_op jit(solution)/shard_map/all_to_all | solution.py:286
  27.1 0.0 copy-start.2
  27.1 0.0 copy-start.3
  27.1 0.7 %copy-done.2 = f32[3]{0:T(128)S(1)} copy-done((f32[3]{0:T(128)S(1)}, f32[3]{0:T(128)}, u32[]{:S(2)}) %copy-start.2) | copy-done | bytes 36
  27.8 0.0 copy-done.3
  27.8 1.6 %step.1 = f32[2,3,2,2,129]{4,3,2,1,0:T(2,128)} custom-call(s32[64]{0:T(128)S(1)} %copy-done.1, f32[3]{0:T(128)S(1)} %copy-done.2, f32[3]{0:T(128)S(1)} %copy-done.3, bf16[256,128]{1,0:T(8,128)(2,1)S(1)} %bitcast.5, bf16[2,129,128]{2,1,0:T(8,128)(2,1)S(1)} %copy.6.table_ref, f32[2,3,2,2,129]{4,3,2,1,0:T(2,128)S(1)} %copy-done), custom_call_target="tpu_custom_call" | custom-call | tf_op jit(solution)/shard_map/step/pallas_call | solution.py:289
Async XLA Ops:
  0.0 0.9 %copy-start = (f32[2,3,2,2,129]{4,3,2,1,0:T(2,128)S(1)}, f32[2,3,2,2,129]{4,3,2,1,0:T(2,128)}, u32[]{:S(2)}) copy-start(f32[2,3,2,2,129]{4,3,2,1,0:T(2,128)} %state_ref.3) | copy-start | bytes 37156
  0.9 0.7 %copy-start.1 = (s32[64]{0:T(128)S(1)}, s32[64]{0:T(128)}, u32[]{:S(2)}) copy-start(s32[64]{0:T(128)} %low_ref.3) | copy-start | bytes 772
  27.1 0.7 %copy-start.2 = (f32[3]{0:T(128)S(1)}, f32[3]{0:T(128)}, u32[]{:S(2)}) copy-start(f32[3]{0:T(128)} %rate_ref.1) | copy-start | bytes 40
  27.1 0.7 %copy-start.3 = (f32[3]{0:T(128)S(1)}, f32[3]{0:T(128)}, u32[]{:S(2)}) copy-start(f32[3]{0:T(128)} %coupling_ref.1) | copy-start | bytes 40

commit v2 on v1

--- a/solution.py
+++ b/solution.py
@@ -24,6 +24,12 @@
     before = lax.ppermute(last, axis, up)
     after = lax.ppermute(first, axis, down)
     return jnp.concatenate([before, shard, after], axis=dim)
+
+
+def own_lower(low_ref, at):
+    low_row = low_ref[...][None, :]
+    lane = lax.broadcasted_iota(jnp.int32, low_row.shape, 1)
+    return jnp.sum(jnp.where(lane == at, low_row, 0), axis=1, keepdims=True)
 
 
 def row_factors(lower, shape, orders_total):
@@ -95,7 +101,17 @@
 
 
 def synthesis_kernel(
-    dims, low_ref, low_row_ref, state_ref, table_ref, out_ref, high_ref, rest_ref, spread_ref
+    dims,
+    low_ref,
+    rate_ref,
+    coupling_ref,
+    state_ref,
+    table_ref,
+    out_ref,
+    high_ref,
+    rest_ref,
+    factor_ref,
+    spread_ref,
 ):
     pairs_dev, block, mode_count, orders_total = dims
     fields = state_ref.shape[1]
@@ -104,7 +120,7 @@
     group = lax.axis_index("mode") * pairs_dev
     pieces = []
     for pair in range(pairs_dev):
-        lower = low_ref[group + pair]
+        lower = own_lower(low_ref, group + pair)
         members, signs = row_factors(lower, (1, rows_total), orders_total)
         coeffs = [state_rows(state_ref, pair, part, (*range(fields), 0)) for part in range(2)]
         left = []
@@ -129,7 +145,14 @@
             merged = jnp.where(lane_block == i, moved, merged)
         spread_ref[:, row, :] = merged
     out_ref[...] = spread_ref[...].reshape(out_ref.shape).astype(jnp.bfloat16)
-    fill_waves(low_row_ref[...].astype(jnp.float32), orders_total, high_ref, rest_ref, 32)
+    rows = factor_ref.shape[1]
+    at = lax.broadcasted_iota(jnp.int32, (rows, LANES), 0) // (rows // (fields + 1))
+    for k, ref in enumerate((rate_ref, coupling_ref)):
+        values = ref[...][None, :]
+        factor = jnp.broadcast_to(values[:, 0:1], (rows, LANES))
+        factor = jnp.where(at == 1, values[:, 2:3], factor)
+        factor_ref[k] = jnp.where(at == 2, values[:, 1:2], factor)
+    fill_waves(low_ref[...][None, :].astype(jnp.float32), orders_total, high_ref, rest_ref, 32)
 
 
 def product_kernel(dims, sent_ref, high_ref, rest_ref, out_ref):
@@ -168,7 +191,7 @@
     per_pair = returned.shape[0] // pairs_dev
     half = block // 2
     for pair in range(pairs_dev):
-        lower = low_ref[group + pair]
+        lower = own_lower(low_ref, group + pair)
         members, signs = row_factors(lower, (1, rows_total), orders_total)
         sums = lax.dot_general(
             returned[pair * per_pair : (pair + 1) * per_pair],
@@ -194,7 +217,7 @@
 
 
 def step_kernel(
-    dims, low_ref, rate_ref, coupling_ref, sent_ref, table_ref, state_ref, out_ref, spread_ref
+    dims, low_ref, factor_ref, sent_ref, table_ref, state_ref, out_ref, spread_ref
 ):
     orders_total = dims[-1]
     rows_total = table_ref.shape[1]
@@ -202,17 +225,11 @@
     fields = (0, 2, 1, 0)
     at = lax.broadcasted_iota(jnp.int32, (half, 1), 0)
     upper = at % 2 == 1
-    by_field = [at // 2 == 1, at // 2 == 2]
-
-    def column(ref):
-        first = jnp.full((half, 1), ref[0], jnp.float32)
-        return jnp.where(by_field[0], ref[2], jnp.where(by_field[1], ref[1], first))
-
     def other(value):
         return jnp.where(upper, pltpu.roll(value, 1, 0), pltpu.roll(value, half - 1, 0))
 
-    rate = column(rate_ref)
-    strength = column(coupling_ref)
+    rate = factor_ref[0, :, 0:1]
+    strength = factor_ref[1, :, 0:1]
     radius = inner_radius + (jnp.where(upper, 1.0, 0.0) + 0.5) * shell_step
     inverse = (shell_step * shell_step) / (radius * radius)
     row = lax.broadcasted_iota(jnp.int32, (1, rows_total), 1)
@@ -260,20 +277,19 @@
     used = count * block
     assert half == 8 and chunk_rows * block == LANES and used <= LANES // 2 and part_count == 2
     scale = 2.0 * math.sqrt(orders_total * rows_total / (lat_total * lon_total))
-    low_orders = low_orders.astype(jnp.int32)
-    smem = pl.BlockSpec(memory_space=pltpu.SMEM)
     spread = pltpu.VMEM((mode_count, chunk_rows, LANES), jnp.float32)
     sent = jax.ShapeDtypeStruct((column_count, LANES), jnp.bfloat16)
     table_shape = jax.ShapeDtypeStruct((column_count, lon_total), jnp.bfloat16)
-    chunks, wave_high, wave_rest = pl.pallas_call(
+    factor_shape = jax.ShapeDtypeStruct((2, half, LANES), jnp.float32)
+    chunks, wave_high, wave_rest, factors = pl.pallas_call(
         functools.partial(synthesis_kernel, (pairs_dev, block, mode_count, orders_total)),
-        out_shape=[sent, table_shape, table_shape],
-        in_specs=[smem] + vmem(3),
-        out_specs=vmem(3),
+        out_shape=[sent, table_shape, table_shape, factor_shape],
+        in_specs=vmem(5),
+        out_specs=vmem(4),
         scratch_shapes=[spread],
         compiler_params=GRANT,
         name="synthesis",
-    )(low_orders, low_orders[None, :], spectral_state, synthesis_table)
+    )(low_orders, diffusion, coupling, spectral_state, synthesis_table)
     pieces = lax.all_to_all(chunks, "mode", split_axis=0, concat_axis=0, tiled=True)
     answers = pl.pallas_call(
         functools.partial(product_kernel, (used, shell_count, scale)),
@@ -289,16 +305,16 @@
         return pl.pallas_call(
             functools.partial(step_kernel, dims),
             out_shape=jax.ShapeDtypeStruct(spectral_state.shape, jnp.float32),
-            in_specs=[smem] * 3 + vmem(3),
+            in_specs=vmem(5),
             out_specs=pl.BlockSpec(memory_space=pltpu.VMEM),
             scratch_shapes=[spread],
             compiler_params=GRANT,
             name="step",
-        )(low_orders, diffusion, coupling, returned, synthesis_table, spectral_state)
+        )(low_orders, factors, returned, synthesis_table, spectral_state)
     nonlinear = pl.pallas_call(
         functools.partial(analysis_kernel, dims),
         out_shape=jax.ShapeDtypeStruct((pairs_dev, part_count, half, rows_total), jnp.float32),
-        in_specs=[smem] + vmem(2),
+        in_specs=vmem(3),
         out_specs=pl.BlockSpec(memory_space=pltpu.VMEM),
         scratch_shapes=[spread],
         compiler_params=GRANT,

time: 29.6 us -> 27.3 us (0.922)
  local copies, waits for them, and re-layouts: 2.21 us -> 0.96 us
  Pallas kernels: 3.45 us -> 2.42 us
    unnamed x9, local copies, waits for them, and re-layouts: 2.21 us -> 0.96 us
    pallas_call x1, Pallas kernels: 1.55 us -> 1 us  [body(): pl.pallas_call(functools.partial(step_kernel, dims), out_shape=jax.ShapeD...]
    pallas_call x1, Pallas kernels: 1.33 us -> 0.84 us  [body(): pl.pallas_call(functools.partial(synthesis_kernel, (pairs_dev, block, mod...]
where the time goes in v2:
time: 27.3 us; the launch traced here: 27.1 us
  blocking collectives  23.6 us (86%)
  Pallas kernels  2.42 us (9%)
  local copies, waits for them, and re-layouts  0.96 us (4%)
    all_to_all x1, blocking collectives, body(): lax.all_to_all(chunks, 'mode', split_axis=0, concat_axis=0, tiled=True)  14.5 us
    all_to_all x1, blocking collectives, body(): lax.all_to_all(answers, 'mode', split_axis=0, concat_axis=0, tiled=True)  9.1 us
    pallas_call x1, Pallas kernels, body(): pl.pallas_call(functools.partial(step_kernel, dims), out_shape=jax.ShapeD...  1 us
    unnamed x9, local copies, waits for them, and re-layouts  0.96 us
    pallas_call x1, Pallas kernels, body(): pl.pallas_call(functools.partial(synthesis_kernel, (pairs_dev, block, mod...  0.84 us
    pallas_call x1, Pallas kernels, body(): pl.pallas_call(functools.partial(product_kernel, (used, shell_count, scal...  0.57 us

profile of v2, /device:TPU:0, one launch (start us, length us, event | category | flops | bytes accessed | tf_op | source)
XLA Modules:
  0.0 27.1 jit_solution(11883477746752659859)
XLA Ops:
  0.0 0.0 copy-start.1
  0.0 0.0 copy-start
  0.0 0.0 copy-start.3
  0.0 0.0 copy-start.2
  0.0 0.9 %copy.6.table_ref = bf16[2,129,128]{2,1,0:T(8,128)(2,1)S(1)} copy(bf16[2,129,128]{2,0,1:T(2,128)(2,1)} %param.6) | data formatting | bytes 132096 | tf_op args[1]
  1.0 0.0 copy-done.1
  1.0 0.0 copy-done
  1.0 0.0 copy-done.3
  1.0 0.0 copy-done.2
  1.0 0.8 %synthesis.1 = (bf16[256,128]{1,0:T(8,128)(2,1)S(1)}, bf16[256,384]{1,0:T(8,128)(2,1)S(1)}, bf16[256,384]{1,0:T(8,128)(2,1)S(1)}, f32[2,8,128]{2,1,0:T(8,128)S(1)}) custom-call(s32[64]{0:T(128)S(1)} %copy-done.1, f32[3]{0:T(128)S(1)} %copy-done.2, f32[3]{0:T(128)S(1)} %copy-done.3, f32[2,3,2,2,129]{4,3,2,1,0:T(2,128)S(1)} %copy-done, ...), custom_call_target="tpu_custom_call" | custom-call | tf_op jit(solution)/shard_map/synthesis/pallas_call | solution.py:284
  1.8 14.5 %all_to_all.22 = bf16[32,8,128]{2,1,0:T(8,128)(2,1)S(1)} all-to-all(bf16[32,8,128]{2,1,0:T(8,128)(2,1)S(1)} %bitcast.7), channel_id=1, replica_groups=mesh['radial'=1,'mode'=32] {'mode'}, dimensions={0} | all-to-all | bytes 131072 | tf_op jit(solution)/shard_map/all_to_all | solution.py:293
  16.4 0.6 %products.1 = bf16[256,128]{1,0:T(8,128)(2,1)S(1)} custom-call(bf16[256,128]{1,0:T(8,128)(2,1)S(1)} %bitcast.5, bf16[256,384]{1,0:T(8,128)(2,1)S(1)} %get-tuple-element.11.high_ref, bf16[256,384]{1,0:T(8,128)(2,1)S(1)} %get-tuple-element.12.rest_ref), custom_call_target="tpu_custom_call" | custom-call | tf_op jit(solution)/shard_map/products/pallas_call | solution.py:294
  17.0 9.1 %all_to_all.23 = bf16[32,8,128]{2,1,0:T(8,128)(2,1)S(1)} all-to-all(bf16[32,8,128]{2,1,0:T(8,128)(2,1)S(1)} %bitcast.6), channel_id=1, replica_groups=mesh['radial'=1,'mode'=32] {'mode'}, dimensions={0} | all-to-all | bytes 131072 | tf_op jit(solution)/shard_map/all_to_all | solution.py:302
  26.1 1.0 %step.1 = f32[2,3,2,2,129]{4,3,2,1,0:T(2,128)} custom-call(s32[64]{0:T(128)S(1)} %copy-done.1, f32[2,8,128]{2,1,0:T(8,128)S(1)} %get-tuple-element.9.factor_ref, bf16[256,128]{1,0:T(8,128)(2,1)S(1)} %bitcast.4, bf16[2,129,128]{2,1,0:T(8,128)(2,1)S(1)} %copy.6.table_ref, f32[2,3,2,2,129]{4,3,2,1,0:T(2,128)S(1)} %copy-done), custom_call_target="tpu_custom_call" | custom-call | tf_op jit(solution)/shard_map/step/pallas_call | solution.py:305
Async XLA Ops:
  0.0 1.0 %copy-start.1 = (s32[64]{0:T(128)S(1)}, s32[64]{0:T(128)}, u32[]{:S(2)}) copy-start(s32[64]{0:T(128)} %low_ref.3) | copy-start | bytes 772
  0.0 1.0 %copy-start = (f32[2,3,2,2,129]{4,3,2,1,0:T(2,128)S(1)}, f32[2,3,2,2,129]{4,3,2,1,0:T(2,128)}, u32[]{:S(2)}) copy-start(f32[2,3,2,2,129]{4,3,2,1,0:T(2,128)} %state_ref.3) | copy-start | bytes 37156
  0.0 1.0 %copy-start.3 = (f32[3]{0:T(128)S(1)}, f32[3]{0:T(128)}, u32[]{:S(2)}) copy-start(f32[3]{0:T(128)} %coupling_ref.1) | copy-start | bytes 40
  0.0 1.0 %copy-start.2 = (f32[3]{0:T(128)S(1)}, f32[3]{0:T(128)}, u32[]{:S(2)}) copy-start(f32[3]{0:T(128)} %rate_ref.1) | copy-start | bytes 40

commit v3 on v2

--- a/solution.py
+++ b/solution.py
@@ -259,6 +259,285 @@
     return [pl.BlockSpec(memory_space=pltpu.VMEM)] * count
 
 
+def row_lower(low_ref, first, rows, pairs_dev):
+    at = lax.broadcasted_iota(jnp.int32, (rows, 1), 0)
+    lower = jnp.zeros((rows, 1), jnp.int32)
+    for pair in range(pairs_dev):
+        lower = jnp.where(at // (rows // pairs_dev) == pair, own_lower(low_ref, first + pair), lower)
+    return at, lower
+
+
+def row_members(at, lower, rows_total, orders_total):
+    row = lax.broadcasted_iota(jnp.int32, (1, rows_total), 1)
+    upper = (at // 2) % 2 == 1
+    edge = orders_total - lower
+    member = jnp.logical_xor(row < edge, upper)
+    odd = ((row + jnp.where(upper, edge, 0)) & 1) == 1
+    return member, odd
+
+
+def paired_state(state_ref, field, shell):
+    pairs_dev = state_ref.shape[0]
+    pieces = [state_ref[pair, field, shell] for pair in range(pairs_dev) for _ in range(2)]
+    return jnp.concatenate(pieces, axis=0)
+
+
+def wave_values(turns, lon_total):
+    quad = jnp.floor(turns * (4.0 / lon_total) + 0.5)
+    angle = (turns - quad * (lon_total / 4)) * (2.0 * math.pi / lon_total)
+    square = angle * angle
+    cosine = 1.0 + square * (
+        -0.5 + square * (1.0 / 24 + square * (-1.0 / 720 + square * (1.0 / 40320)))
+    )
+    sine = 1.0 / 120 + square * (-1.0 / 5040 + square * (1.0 / 362880))
+    sine = angle * (1.0 + square * (-1.0 / 6 + square * sine))
+    quad = quad.astype(jnp.int32)
+    swap = (quad & 1) == 1
+    cosine, sine = (jnp.where(swap, sine, cosine), jnp.where(swap, cosine, sine))
+    cosine = jnp.where(((quad + 1) & 2) == 2, -cosine, cosine)
+    sine = jnp.where((quad & 2) == 2, -sine, sine)
+    return cosine, sine
+
+
+def third_factors(order, is_cosine, at):
+    third = math.sqrt(0.75)
+    turn = at * order
+    turn = turn - 3.0 * jnp.floor((turn + 0.5) * (1.0 / 3.0))
+    cos_at = jnp.where(turn == 0.0, 1.0, -0.5)
+    sin_at = jnp.where(turn == 0.0, 0.0, jnp.where(turn == 1.0, third, -third))
+    by_cosine = jnp.where(is_cosine, cos_at, -sin_at)
+    by_sine = jnp.where(is_cosine, -sin_at, -cos_at)
+    return by_cosine, by_sine
+
+
+def two_terms(value):
+    high = value.astype(jnp.bfloat16)
+    return high, (value - high.astype(jnp.float32)).astype(jnp.bfloat16)
+
+
+def band_synthesis_kernel(
+    dims,
+    low_ref,
+    rate_ref,
+    coupling_ref,
+    state_ref,
+    table_ref,
+    out_ref,
+    high_ref,
+    rest_ref,
+    own_ref,
+    factor_ref,
+):
+    group, mode_count, orders_total = dims
+    pairs_dev, fields, shells, _, rows_total = state_ref.shape
+    rows = out_ref.shape[0] // mode_count
+    me = lax.axis_index("mode")
+    at, lower = row_lower(low_ref, me * pairs_dev, rows, pairs_dev)
+    member, odd = row_members(at, lower, rows_total, orders_total)
+    order = jnp.where((at // 2) % 2 == 1, orders_total - 1 - lower, lower)
+    weight = jnp.where(order == 0, 1.0, 2.0)
+    north = jnp.where(member, weight, 0.0)
+    south = jnp.where(odd, -north, north)
+    state = [[paired_state(state_ref, f, s) for f in range(fields)] for s in range(shells)]
+    fourier = None
+    for pair in range(pairs_dev):
+        mine = at // (rows // pairs_dev) == pair
+        left = [
+            state[s][f] * jnp.where(mine, factor, 0.0)
+            for factor in (north, south)
+            for s in range(shells)
+            for f in range(fields)
+        ]
+        left = jnp.concatenate(left, axis=0).astype(jnp.bfloat16)
+        part = jnp.dot(left, table_ref[pair], preferred_element_type=jnp.float32)
+        fourier = part if fourier is None else fourier + part
+    fourier = fourier.astype(jnp.bfloat16).astype(jnp.float32)
+    width = LANES // group
+    lane_block = lax.broadcasted_iota(jnp.int32, (fields * rows, LANES), 1) // width
+    for band in range(group):
+        piece = None
+        for block in range(group):
+            source = fourier[block * fields * rows : (block + 1) * fields * rows]
+            moved = pltpu.roll(source, (width * (block - band)) % LANES, 1)
+            piece = moved if piece is None else jnp.where(lane_block == block, moved, piece)
+        for field in range(fields):
+            value = piece[field * rows : (field + 1) * rows].astype(jnp.bfloat16)
+            for device in range(band, mode_count, group):
+                out_ref[device * rows : (device + 1) * rows, field * LANES : (field + 1) * LANES] = value
+
+    lon_total, columns = high_ref.shape
+    span = lon_total // 3
+    low_row = low_ref[...][None, :].astype(jnp.float32)
+    pair_at = lax.broadcasted_iota(jnp.int32, (low_row.shape[1], columns), 0)
+    column = lax.broadcasted_iota(jnp.int32, (low_row.shape[1], columns), 1)
+    spread = jnp.where(column // 4 == pair_at, 1.0, 0.0).astype(jnp.bfloat16)
+    lowers = jnp.broadcast_to(low_row, (8, low_row.shape[1])).astype(jnp.bfloat16)
+    lowers = jnp.dot(lowers, spread, preferred_element_type=jnp.float32)[0:1]
+    column = lax.broadcasted_iota(jnp.int32, (1, columns), 1)
+    orders = jnp.where((column // 2) % 2 == 0, lowers, orders_total - 1 - lowers)
+    is_cosine = column % 2 == 0
+    factors = [third_factors(orders, is_cosine, third) for third in range(3)]
+    step = min(span, 32)
+    for base in range(0, span, step):
+        lon = (base + lax.broadcasted_iota(jnp.int32, (step, 1), 0)).astype(jnp.float32)
+        cosine, sine = wave_values(lon * orders, lon_total)
+        for third, (by_cosine, by_sine) in enumerate(factors):
+            high, rest = two_terms(cosine * by_cosine + sine * by_sine)
+            high_ref[third * span + base : third * span + base + step, :] = high
+            rest_ref[third * span + base : third * span + base + step, :] = rest
+    count = group * rows
+    at = lax.broadcasted_iota(jnp.int32, (count, 1), 0)
+    device = me - me % group + ((me % group) ^ (at // rows))
+    pair_index = device * pairs_dev + (at % rows) // 4
+    pair_lane = lax.broadcasted_iota(jnp.int32, (count, low_row.shape[1]), 1)
+    lowers = jnp.sum(jnp.where(pair_lane == pair_index, low_row, 0.0), axis=1, keepdims=True)
+    orders = jnp.where((at // 2) % 2 == 0, lowers, orders_total - 1 - lowers)
+    is_cosine = at % 2 == 0
+    lon = lax.broadcasted_iota(jnp.int32, (1, span), 1).astype(jnp.float32)
+    cosine, sine = wave_values(lon * orders, lon_total)
+    for third in range(3):
+        by_cosine, by_sine = third_factors(orders, is_cosine, third)
+        high, rest = two_terms(cosine * by_cosine + sine * by_sine)
+        own_ref[:count, third * span : (third + 1) * span] = high
+        own_ref[count:, third * span : (third + 1) * span] = rest
+    for k, ref in enumerate((rate_ref, coupling_ref)):
+        for f in range(fields):
+            factor_ref[k, f] = jnp.broadcast_to(ref[...][None, f : f + 1], (8, LANES))
+
+
+def band_product_kernel(scale, sent_ref, high_ref, rest_ref, own_ref, *out_refs):
+    sent = sent_ref[...]
+    grid = jnp.dot(high_ref[...], sent, preferred_element_type=jnp.float32)
+    grid = grid + jnp.dot(rest_ref[...], sent, preferred_element_type=jnp.float32)
+    width = sent.shape[1] // 3
+    first, second, third = (grid[:, f * width : (f + 1) * width] for f in range(3))
+    products = jnp.concatenate([first * second, first * third, second * third], axis=1)
+    high, rest = two_terms(products)
+    count = own_ref.shape[0] // 2
+    both = jnp.dot(own_ref[...], high, preferred_element_type=jnp.float32)
+    totals = jnp.dot(own_ref[:count], rest, preferred_element_type=jnp.float32)
+    totals = totals + both[:count] + both[count:]
+    answers = (totals * scale).astype(jnp.bfloat16)
+    rows = count // len(out_refs)
+    for at, out_ref in enumerate(out_refs):
+        out_ref[...] = answers[at * rows : (at + 1) * rows]
+
+
+def band_step_kernel(dims, low_ref, factor_ref, state_ref, table_ref, *refs):
+    group, orders_total = dims
+    sent_refs, out_ref = (refs[:group], refs[group])
+    pairs_dev, fields, shells, _, rows_total = state_ref.shape
+    rows = sent_refs[0].shape[0]
+    me = lax.axis_index("mode")
+    at, lower = row_lower(low_ref, me * pairs_dev, rows, pairs_dev)
+    member, odd = row_members(at, lower, rows_total, orders_total)
+    width = LANES // group
+    lane_block = lax.broadcasted_iota(jnp.int32, (fields * rows, LANES), 1) // width
+    pieces = []
+    for ref in sent_refs:
+        value = ref[...].astype(jnp.float32)
+        pieces.append(
+            jnp.concatenate([value[:, f * LANES : (f + 1) * LANES] for f in range(fields)], axis=0)
+        )
+    returned = []
+    for block in range(group):
+        merged = jnp.zeros((fields * rows, LANES), jnp.float32)
+        for mask, piece in enumerate(pieces):
+            band = (me % group) ^ mask
+            moved = pltpu.roll(piece, (width * (band - block + group)) % LANES, 1)
+            merged = jnp.where(lane_block == band, moved, merged)
+        returned.append(merged)
+    returned = jnp.concatenate(returned, axis=0).astype(jnp.bfloat16)
+    sums = [
+        lax.dot_general(returned, table_ref[pair], NT, preferred_element_type=jnp.float32)
+        for pair in range(pairs_dev)
+    ]
+    row = lax.broadcasted_iota(jnp.int32, (1, rows_total), 1)
+    degree = jnp.where(row < orders_total - lower, lower + row, row - 1).astype(jnp.float32)
+    degree = degree * (degree + 1.0)
+    damping = []
+    for s in range(shells):
+        radius = inner_radius + (s + 0.5) * shell_step
+        damping.append(degree * (shell_step * shell_step / (radius * radius)))
+    by_pair = at // (rows // pairs_dev)
+    for f in range(fields):
+        rate = factor_ref[0, f, :, 0:1]
+        strength = factor_ref[1, f, :, 0:1]
+        state, drive, diagonal = ([], [], [])
+        for s in range(shells):
+            state.append(paired_state(state_ref, f, s))
+            diagonal.append(1.0 + rate * (2.0 + damping[s]))
+        for s in range(shells):
+            halves = []
+            for h in range(2):
+                start = ((h * shells + s) * fields + f) * rows
+                value = sums[0][start : start + rows]
+                for pair in range(1, pairs_dev):
+                    value = jnp.where(by_pair == pair, sums[pair][start : start + rows], value)
+                halves.append(value)
+            total = halves[0] + jnp.where(odd, -halves[1], halves[1])
+            total = jnp.where(member, total, 0.0)
+            total = total + pltpu.roll(total, rows - 2, 0)
+            laplace = state[1 - s] - 2.0 * state[s] - damping[s] * state[s]
+            drive.append(state[s] + rate * (laplace + strength * total))
+        factor = 1.0 / (diagonal[0] * diagonal[1] - rate * rate)
+        for s in range(shells):
+            updated = (diagonal[1 - s] * drive[s] + rate * drive[1 - s]) * factor
+            for pair in range(pairs_dev):
+                start = pair * (rows // pairs_dev)
+                out_ref[pair, f, s] = updated[start : start + 2]
+
+
+def banded(group, spectral_state, synthesis_table, low_orders, diffusion, coupling):
+    pairs_dev, field_count, shell_count, part_count, rows_total = spectral_state.shape
+    half_lat = synthesis_table.shape[2]
+    orders_total = rows_total - 1
+    lon_total = 3 * orders_total
+    mode_count = lax.axis_size("mode")
+    rows = pairs_dev * 2 * part_count
+    columns = rows * mode_count
+    scale = 2.0 * math.sqrt(orders_total * rows_total / (2 * half_lat * lon_total))
+
+    def like(shape, dtype=jnp.bfloat16):
+        return jax.ShapeDtypeStruct(shape, dtype)
+
+    chunks, wave_high, wave_rest, own_waves, factors = pl.pallas_call(
+        functools.partial(band_synthesis_kernel, (group, mode_count, orders_total)),
+        out_shape=[
+            like((columns, field_count * LANES)),
+            like((lon_total, columns)),
+            like((lon_total, columns)),
+            like((2 * group * rows, lon_total)),
+            like((2, field_count, 8, LANES), jnp.float32),
+        ],
+        in_specs=vmem(5),
+        out_specs=vmem(5),
+        compiler_params=GRANT,
+        name="synthesis",
+    )(low_orders, diffusion, coupling, spectral_state, synthesis_table)
+    pieces = lax.all_to_all(chunks, "mode", split_axis=0, concat_axis=0, tiled=True)
+    answers = pl.pallas_call(
+        functools.partial(band_product_kernel, scale),
+        out_shape=[like((rows, field_count * LANES))] * group,
+        in_specs=vmem(4),
+        out_specs=vmem(group),
+        compiler_params=GRANT,
+        name="products",
+    )(pieces, wave_high, wave_rest, own_waves)
+    returned = [answers[0]]
+    for mask in range(1, group):
+        ring = [(i, i ^ mask) for i in range(mode_count)]
+        returned.append(lax.ppermute(answers[mask], "mode", ring))
+    return pl.pallas_call(
+        functools.partial(band_step_kernel, (group, orders_total)),
+        out_shape=like(spectral_state.shape, jnp.float32),
+        in_specs=vmem(4 + group),
+        out_specs=pl.BlockSpec(memory_space=pltpu.VMEM),
+        compiler_params=GRANT,
+        name="step",
+    )(low_orders, factors, spectral_state, synthesis_table, *returned)
+
+
 def body(spectral_state, synthesis_table, low_orders, diffusion, coupling):
     radial_count = lax.axis_size("radial")
     if radial_count > 1:
@@ -277,6 +556,9 @@
     used = count * block
     assert half == 8 and chunk_rows * block == LANES and used <= LANES // 2 and part_count == 2
     scale = 2.0 * math.sqrt(orders_total * rows_total / (lat_total * lon_total))
+    group = 2 * shell_count * half_lat // LANES
+    if radial_count == 1 and shell_count == 2 and group == 4 and mode_count % group == 0:
+        return banded(group, spectral_state, synthesis_table, low_orders, diffusion, coupling)
     spread = pltpu.VMEM((mode_count, chunk_rows, LANES), jnp.float32)
     sent = jax.ShapeDtypeStruct((column_count, LANES), jnp.bfloat16)
     table_shape = jax.ShapeDtypeStruct((column_count, lon_total), jnp.bfloat16)

time: 27.3 us -> 23.5 us (0.86)
  blocking collectives: 23.6 us -> 16.1 us
  waiting for transfers between devices: 0 us -> 2.2 us
  starting transfers between devices: 0 us -> 2 us
  Pallas kernels: 2.42 us -> 2 us
    all_to_all x2 -> x1, blocking collectives: 23.6 us -> 16.1 us  [banded(): lax.all_to_all(chunks, 'mode', split_axis=0, concat_axis=0, tiled=True)]
    ppermute x0 -> x3, waiting for transfers between devices: none -> 2.2 us  [banded(): returned.append(lax.ppermute(answers[mask], 'mode', ring))]
    ppermute x0 -> x3, starting transfers between devices: none -> 2 us  [banded(): returned.append(lax.ppermute(answers[mask], 'mode', ring))]
    pallas_call x3, Pallas kernels: 2.42 us -> 2 us  [the longest x1 0.9 us: banded(): pl.pallas_call(functools.partial(band_step_kernel, (group, orders_total))...]
  transfers between devices with their start and end apart: 0 -> 3, of which waited for: 0 -> 1; matrix products, arithmetic and copies ran while one was open for 0% -> 0% of each run, Pallas kernels for 0% -> 0%
where the time goes in v3:
time: 23.5 us; the launch traced here: 23.3 us
  blocking collectives  16.1 us (69%)
  waiting for transfers between devices  2.2 us (9%)
  Pallas kernels  2 us (9%)
  starting transfers between devices  2 us (9%)
  local copies, waits for them, and re-layouts  0.96 us (4%)
    all_to_all x1, blocking collectives, banded(): lax.all_to_all(chunks, 'mode', split_axis=0, concat_axis=0, tiled=True)  16.1 us
    ppermute x3, waiting for transfers between devices, banded(): returned.append(lax.ppermute(answers[mask], 'mode', ring))  2.2 us
    ppermute x3, starting transfers between devices, banded(): returned.append(lax.ppermute(answers[mask], 'mode', ring))  2 us
    unnamed x9, local copies, waits for them, and re-layouts  0.96 us
    pallas_call x1, Pallas kernels, banded(): pl.pallas_call(functools.partial(band_step_kernel, (group, orders_total))...  0.9 us
    pallas_call x1, Pallas kernels, banded(): pl.pallas_call(functools.partial(band_synthesis_kernel, (group, mode_coun...  0.56 us
    pallas_call x1, Pallas kernels, banded(): pl.pallas_call(functools.partial(band_product_kernel, scale), out_shape=[...  0.54 us
  transfers between devices with their start and end apart: 3, of which 1 were waited for; matrix products, arithmetic and copies ran while one was open for 0% of the time, Pallas kernels for 0%

profile of v3, /device:TPU:0, one launch (start us, length us, event | category | flops | bytes accessed | tf_op | source)
XLA Modules:
  0.0 23.3 jit_solution(16039849842503406160)
XLA Ops:
  0.0 0.0 copy-start.1
  0.0 0.0 copy-start
  0.0 0.0 copy-start.3
  0.0 0.0 copy-start.2
  0.0 0.9 %copy.6.table_ref = bf16[2,129,128]{2,1,0:T(8,128)(2,1)S(1)} copy(bf16[2,129,128]{2,0,1:T(2,128)(2,1)} %param.6) | data formatting | bytes 132096 | tf_op args[1]
  1.0 0.0 copy-done.1
  1.0 0.0 copy-done
  1.0 0.0 copy-done.3
  1.0 0.0 copy-done.2
  1.0 0.6 %synthesis.1 = (bf16[256,384]{1,0:T(8,128)(2,1)S(1)}, bf16[384,256]{1,0:T(8,128)(2,1)S(1)}, bf16[384,256]{1,0:T(8,128)(2,1)S(1)}, bf16[64,384]{1,0:T(8,128)(2,1)S(1)}, f32[2,3,8,128]{3,2,1,0:T(8,128)S(1)}) custom-call(s32[64]{0:T(128)S(1)} %copy-done.1, f32[3]{0:T(128)S(1)} %copy-done.2, f32[3]{0:T(128)S(1)} %copy-done.3, f32[2,3,2,2,129]{4,3,2,1,0:T(2,128)S(1)} %copy-done, ...), custom_call_target="tpu_custom_call" | custom-call | tf_op jit(solution)/shard_map/synthesis/pallas_call | solution.py:504
  1.6 16.1 %all_to_all.11 = bf16[32,8,384]{2,1,0:T(8,128)(2,1)S(1)} all-to-all(bf16[32,8,384]{2,1,0:T(8,128)(2,1)S(1)} %bitcast.3), channel_id=1, replica_groups=mesh['radial'=1,'mode'=32] {'mode'}, dimensions={0} | all-to-all | bytes 393216 | tf_op jit(solution)/shard_map/all_to_all | solution.py:518
  17.7 0.5 %products.1 = (bf16[8,384]{1,0:T(8,128)(2,1)S(1)}, bf16[8,384]{1,0:T(8,128)(2,1)S(1)}, bf16[8,384]{1,0:T(8,128)(2,1)S(1)}, bf16[8,384]{1,0:T(8,128)(2,1)S(1)}) custom-call(bf16[256,384]{1,0:T(8,128)(2,1)S(1)} %bitcast.2, bf16[384,256]{1,0:T(8,128)(2,1)S(1)} %get-tuple-element.16.high_ref, bf16[384,256]{1,0:T(8,128)(2,1)S(1)} %get-tuple-element.17.rest_ref, ...), custom_call_target="tpu_custom_call" | custom-call | tf_op jit(solution)/shard_map/products/pallas_call | solution.py:519
  18.2 0.6 %collective-permute-start = (bf16[8,384]{1,0:T(8,128)(2,1)S(1)}, bf16[8,384]{1,0:T(8,128)(2,1)S(1)}, u32[]{:S(2)}, u32[]{:S(2)}) collective-permute-start(bf16[8,384]{1,0:T(8,128)(2,1)S(1)} %get-tuple-element.20), channel_id=1, source_target_pairs={{0,1},{1,0},{2,3},{3,2},{4,5},{5,4},{6,7},{7,6},{8,9},{9,8},{10,11... | collective-permute-start | bytes 18440 | tf_op jit(solution)/shard_map/ppermute | solution.py:530
  18.8 0.4 %collective-permute-start.1 = (bf16[8,384]{1,0:T(8,128)(2,1)S(1)}, bf16[8,384]{1,0:T(8,128)(2,1)S(1)}, u32[]{:S(2)}, u32[]{:S(2)}) collective-permute-start(bf16[8,384]{1,0:T(8,128)(2,1)S(1)} %get-tuple-element.21), channel_id=1, source_target_pairs={{0,2},{1,3},{2,0},{3,1},{4,6},{5,7},{6,4},{7,5},{8,10},{9,11},{10,... | collective-permute-start | bytes 18440 | tf_op jit(solution)/shard_map/ppermute | solution.py:530
  19.2 1.0 %collective-permute-start.2 = (bf16[8,384]{1,0:T(8,128)(2,1)S(1)}, bf16[8,384]{1,0:T(8,128)(2,1)S(1)}, u32[]{:S(2)}, u32[]{:S(2)}) collective-permute-start(bf16[8,384]{1,0:T(8,128)(2,1)S(1)} %get-tuple-element.22), channel_id=1, source_target_pairs={{0,3},{1,2},{2,1},{3,0},{4,7},{5,6},{6,5},{7,4},{8,11},{9,10},{10,... | collective-permute-start | bytes 18440 | tf_op jit(solution)/shard_map/ppermute | solution.py:530
  20.2 0.0 collective-permute-done.refs_1_
  20.2 2.2 %collective-permute-done.1.refs_2_ = bf16[8,384]{1,0:T(8,128)(2,1)S(1)} collective-permute-done((bf16[8,384]{1,0:T(8,128)(2,1)S(1)}, bf16[8,384]{1,0:T(8,128)(2,1)S(1)}, u32[]{:S(2)}, u32[]{:S(2)}) %collective-permute-start.1) | collective-permute-done | bytes 6176 | tf_op jit(solution)/shard_map/ppermute | solution.py:530
  22.4 0.0 collective-permute-done.2.refs_3_
  22.4 0.9 %step.1 = f32[2,3,2,2,129]{4,3,2,1,0:T(2,128)} custom-call(s32[64]{0:T(128)S(1)} %copy-done.1, f32[2,3,8,128]{3,2,1,0:T(8,128)S(1)} %get-tuple-element.14.factor_ref, f32[2,3,2,2,129]{4,3,2,1,0:T(2,128)S(1)} %copy-done, bf16[2,129,128]{2,1,0:T(8,128)(2,1)S(1)} %copy.6.table_ref, bf16[8,384]{1,0:T(8,128)(2,1)S(1)} %get-tuple-element.19.refs_0_, ...), custom_call_target="tpu_custom_call" | custom-call | tf_op jit(solution)/shard_map/step/pallas_call | solution.py:531
Async XLA Ops:
  0.0 1.0 %copy-start.1 = (s32[64]{0:T(128)S(1)}, s32[64]{0:T(128)}, u32[]{:S(2)}) copy-start(s32[64]{0:T(128)} %low_ref.3) | copy-start | bytes 772
  0.0 1.0 %copy-start = (f32[2,3,2,2,129]{4,3,2,1,0:T(2,128)S(1)}, f32[2,3,2,2,129]{4,3,2,1,0:T(2,128)}, u32[]{:S(2)}) copy-start(f32[2,3,2,2,129]{4,3,2,1,0:T(2,128)} %state_ref.3) | copy-start | bytes 37156
  0.0 1.0 %copy-start.3 = (f32[3]{0:T(128)S(1)}, f32[3]{0:T(128)}, u32[]{:S(2)}) copy-start(f32[3]{0:T(128)} %coupling_ref.1) | copy-start | bytes 40
  0.0 1.0 %copy-start.2 = (f32[3]{0:T(128)S(1)}, f32[3]{0:T(128)}, u32[]{:S(2)}) copy-start(f32[3]{0:T(128)} %rate_ref.1) | copy-start | bytes 40
  18.2 2.0 %collective-permute-start = (bf16[8,384]{1,0:T(8,128)(2,1)S(1)}, bf16[8,384]{1,0:T(8,128)(2,1)S(1)}, u32[]{:S(2)}, u32[]{:S(2)}) collective-permute-start(bf16[8,384]{1,0:T(8,128)(2,1)S(1)} %get-tuple-element.20), channel_id=1, source_target_pairs={{0,1},{1,0},{2,3},{3,2},{4,5},{5,4},{6,7},{7,6},{8,9},{9,8},{10,11... | collective-permute-start | bytes 18440 | tf_op jit(solution)/shard_map/ppermute | solution.py:530
  18.8 3.6 %collective-permute-start.1 = (bf16[8,384]{1,0:T(8,128)(2,1)S(1)}, bf16[8,384]{1,0:T(8,128)(2,1)S(1)}, u32[]{:S(2)}, u32[]{:S(2)}) collective-permute-start(bf16[8,384]{1,0:T(8,128)(2,1)S(1)} %get-tuple-element.21), channel_id=1, source_target_pairs={{0,2},{1,3},{2,0},{3,1},{4,6},{5,7},{6,4},{7,5},{8,10},{9,11},{10,... | collective-permute-start | bytes 18440 | tf_op jit(solution)/shard_map/ppermute | solution.py:530
  19.2 3.2 %collective-permute-start.2 = (bf16[8,384]{1,0:T(8,128)(2,1)S(1)}, bf16[8,384]{1,0:T(8,128)(2,1)S(1)}, u32[]{:S(2)}, u32[]{:S(2)}) collective-permute-start(bf16[8,384]{1,0:T(8,128)(2,1)S(1)} %get-tuple-element.22), channel_id=1, source_target_pairs={{0,3},{1,2},{2,1},{3,0},{4,7},{5,6},{6,5},{7,4},{8,11},{9,10},{10,... | collective-permute-start | bytes 18440 | tf_op jit(solution)/shard_map/ppermute | solution.py:530

commit v4 on v3

--- a/solution.py
+++ b/solution.py
@@ -8,9 +8,12 @@
 from jax.experimental.pallas import tpu as pltpu
 from jax.sharding import PartitionSpec as P
 
+
 inner_radius = 0.538
 shell_step = 1.0 / 2048.0
 LANES = 128
+SLOT_STEP = 11
+SLOT_FLIP = 29
 GRANT = pltpu.CompilerParams(vmem_limit_bytes=16 * 1024 * 1024)
 NT = (((1,), (1,)), ((), ()))
 
@@ -225,6 +228,7 @@
     fields = (0, 2, 1, 0)
     at = lax.broadcasted_iota(jnp.int32, (half, 1), 0)
     upper = at % 2 == 1
+
     def other(value):
         return jnp.where(upper, pltpu.roll(value, 1, 0), pltpu.roll(value, half - 1, 0))
 
@@ -313,6 +317,18 @@
 def two_terms(value):
     high = value.astype(jnp.bfloat16)
     return high, (value - high.astype(jnp.float32)).astype(jnp.bfloat16)
+
+
+def slot_device(slot, mode_count):
+    return ((SLOT_STEP * slot) ^ SLOT_FLIP) & (mode_count - 1)
+
+
+def band_of(device, mode_count):
+    return (device & 1) | (((device // (mode_count // 4)) & 1) << 1)
+
+
+def member_step(mask, mode_count):
+    return (mask & 1) | ((mask >> 1) * (mode_count // 4))
 
 
 def band_synthesis_kernel(
@@ -362,15 +378,17 @@
             piece = moved if piece is None else jnp.where(lane_block == block, moved, piece)
         for field in range(fields):
             value = piece[field * rows : (field + 1) * rows].astype(jnp.bfloat16)
-            for device in range(band, mode_count, group):
-                out_ref[device * rows : (device + 1) * rows, field * LANES : (field + 1) * LANES] = value
+            for slot in range(mode_count):
+                if band_of(slot_device(slot, mode_count), mode_count) == band:
+                    out_ref[slot * rows : (slot + 1) * rows, field * LANES : (field + 1) * LANES] = value
 
     lon_total, columns = high_ref.shape
     span = lon_total // 3
     low_row = low_ref[...][None, :].astype(jnp.float32)
     pair_at = lax.broadcasted_iota(jnp.int32, (low_row.shape[1], columns), 0)
     column = lax.broadcasted_iota(jnp.int32, (low_row.shape[1], columns), 1)
-    spread = jnp.where(column // 4 == pair_at, 1.0, 0.0).astype(jnp.bfloat16)
+    device = slot_device(column // rows, mode_count)
+    spread = jnp.where(device * pairs_dev + (column % rows) // 4 == pair_at, 1.0, 0.0).astype(jnp.bfloat16)
     lowers = jnp.broadcast_to(low_row, (8, low_row.shape[1])).astype(jnp.bfloat16)
     lowers = jnp.dot(lowers, spread, preferred_element_type=jnp.float32)[0:1]
     column = lax.broadcasted_iota(jnp.int32, (1, columns), 1)
@@ -387,7 +405,7 @@
             rest_ref[third * span + base : third * span + base + step, :] = rest
     count = group * rows
     at = lax.broadcasted_iota(jnp.int32, (count, 1), 0)
-    device = me - me % group + ((me % group) ^ (at // rows))
+    device = me ^ member_step(at // rows, mode_count)
     pair_index = device * pairs_dev + (at % rows) // 4
     pair_lane = lax.broadcasted_iota(jnp.int32, (count, low_row.shape[1]), 1)
     lowers = jnp.sum(jnp.where(pair_lane == pair_index, low_row, 0.0), axis=1, keepdims=True)
@@ -424,7 +442,7 @@
 
 
 def band_step_kernel(dims, low_ref, factor_ref, state_ref, table_ref, *refs):
-    group, orders_total = dims
+    group, mode_count, orders_total = dims
     sent_refs, out_ref = (refs[:group], refs[group])
     pairs_dev, fields, shells, _, rows_total = state_ref.shape
     rows = sent_refs[0].shape[0]
@@ -443,7 +461,7 @@
     for block in range(group):
         merged = jnp.zeros((fields * rows, LANES), jnp.float32)
         for mask, piece in enumerate(pieces):
-            band = (me % group) ^ mask
+            band = band_of(me, mode_count) ^ mask
             moved = pltpu.roll(piece, (width * (band - block + group)) % LANES, 1)
             merged = jnp.where(lane_block == band, moved, merged)
         returned.append(merged)
@@ -489,7 +507,7 @@
 
 
 def banded(group, spectral_state, synthesis_table, low_orders, diffusion, coupling):
-    pairs_dev, field_count, shell_count, part_count, rows_total = spectral_state.shape
+    pairs_dev, field_count, _, part_count, rows_total = spectral_state.shape
     half_lat = synthesis_table.shape[2]
     orders_total = rows_total - 1
     lon_total = 3 * orders_total
@@ -515,7 +533,10 @@
         compiler_params=GRANT,
         name="synthesis",
     )(low_orders, diffusion, coupling, spectral_state, synthesis_table)
-    pieces = lax.all_to_all(chunks, "mode", split_axis=0, concat_axis=0, tiled=True)
+    slots = [slot_device(slot, mode_count) for slot in range(mode_count)]
+    pieces = lax.all_to_all(
+        chunks, "mode", split_axis=0, concat_axis=0, tiled=True, axis_index_groups=[slots]
+    )
     answers = pl.pallas_call(
         functools.partial(band_product_kernel, scale),
         out_shape=[like((rows, field_count * LANES))] * group,
@@ -526,10 +547,10 @@
     )(pieces, wave_high, wave_rest, own_waves)
     returned = [answers[0]]
     for mask in range(1, group):
-        ring = [(i, i ^ mask) for i in range(mode_count)]
+        ring = [(i, i ^ member_step(mask, mode_count)) for i in range(mode_count)]
         returned.append(lax.ppermute(answers[mask], "mode", ring))
     return pl.pallas_call(
-        functools.partial(band_step_kernel, (group, orders_total)),
+        functools.partial(band_step_kernel, (group, mode_count, orders_total)),
         out_shape=like(spectral_state.shape, jnp.float32),
         in_specs=vmem(4 + group),
         out_specs=pl.BlockSpec(memory_space=pltpu.VMEM),
@@ -557,7 +578,7 @@
     assert half == 8 and chunk_rows * block == LANES and used <= LANES // 2 and part_count == 2
     scale = 2.0 * math.sqrt(orders_total * rows_total / (lat_total * lon_total))
     group = 2 * shell_count * half_lat // LANES
-    if radial_count == 1 and shell_count == 2 and group == 4 and mode_count % group == 0:
+    if radial_count == 1 and shell_count == 2 and group == 4 and mode_count >= 8 and mode_count & (mode_count - 1) == 0:
         return banded(group, spectral_state, synthesis_table, low_orders, diffusion, coupling)
     spread = pltpu.VMEM((mode_count, chunk_rows, LANES), jnp.float32)
     sent = jax.ShapeDtypeStruct((column_count, LANES), jnp.bfloat16)
@@ -609,7 +630,7 @@
 
 
 def solve(spectral_state, nonlinear, low_orders, diffusion, coupling):
-    pairs_dev, field_count, shell_count, part_count, rows_total = spectral_state.shape
+    pairs_dev, field_count, shell_count, _, rows_total = spectral_state.shape
     orders_total = rows_total - 1
     radial_count = lax.axis_size("radial")
     own = lax.dynamic_slice_in_dim(low_orders, lax.axis_index("mode") * pairs_dev, pairs_dev)

time: 23.5 us -> 22.4 us (0.953)
  blocking collectives: 16.1 us -> 15.1 us
    all_to_all x1, blocking collectives: 16.1 us -> 15.1 us  [banded(): lax.all_to_all(chunks, 'mode', split_axis=0, concat_axis=0, tiled=True, a...]
  transfers between devices with their start and end apart: 3 -> 3, of which waited for: 1 -> 2; matrix products, arithmetic and copies ran while one was open for 0% -> 0% of each run, Pallas kernels for 0% -> 0%
where the time goes in v4:
time: 22.4 us; the launch traced here: 22.2 us
  blocking collectives  15.1 us (67%)
  waiting for transfers between devices  2.16 us (10%)
  Pallas kernels  2 us (9%)
  starting transfers between devices  1.93 us (9%)
  local copies, waits for them, and re-layouts  0.96 us (4%)
    all_to_all x1, blocking collectives, banded(): lax.all_to_all(chunks, 'mode', split_axis=0, concat_axis=0, tiled=True, a...  15.1 us
    ppermute x3, waiting for transfers between devices, banded(): returned.append(lax.ppermute(answers[mask], 'mode', ring))  2.16 us
    ppermute x3, starting transfers between devices, banded(): returned.append(lax.ppermute(answers[mask], 'mode', ring))  1.93 us
    unnamed x9, local copies, waits for them, and re-layouts  0.96 us
    pallas_call x1, Pallas kernels, banded(): pl.pallas_call(functools.partial(band_step_kernel, (group, mode_count, or...  0.89 us
    pallas_call x1, Pallas kernels, banded(): pl.pallas_call(functools.partial(band_synthesis_kernel, (group, mode_coun...  0.56 us
    pallas_call x1, Pallas kernels, banded(): pl.pallas_call(functools.partial(band_product_kernel, scale), out_shape=[...  0.54 us
  transfers between devices with their start and end apart: 3, of which 2 were waited for; matrix products, arithmetic and copies ran while one was open for 0% of the time, Pallas kernels for 0%

profile of v4, /device:TPU:0, one launch (start us, length us, event | category | flops | bytes accessed | tf_op | source)
XLA Modules:
  0.0 22.2 jit_solution(9904981085362938826)
XLA Ops:
  0.0 0.0 copy-start.1
  0.0 0.0 copy-start
  0.0 0.0 copy-start.3
  0.0 0.0 copy-start.2
  0.0 0.9 %copy.6.table_ref = bf16[2,129,128]{2,1,0:T(8,128)(2,1)S(1)} copy(bf16[2,129,128]{2,0,1:T(2,128)(2,1)} %param.6) | data formatting | bytes 132096 | tf_op args[1]
  1.0 0.0 copy-done.1
  1.0 0.0 copy-done
  1.0 0.0 copy-done.3
  1.0 0.0 copy-done.2
  1.0 0.6 %synthesis.1 = (bf16[256,384]{1,0:T(8,128)(2,1)S(1)}, bf16[384,256]{1,0:T(8,128)(2,1)S(1)}, bf16[384,256]{1,0:T(8,128)(2,1)S(1)}, bf16[64,384]{1,0:T(8,128)(2,1)S(1)}, f32[2,3,8,128]{3,2,1,0:T(8,128)S(1)}) custom-call(s32[64]{0:T(128)S(1)} %copy-done.1, f32[3]{0:T(128)S(1)} %copy-done.2, f32[3]{0:T(128)S(1)} %copy-done.3, f32[2,3,2,2,129]{4,3,2,1,0:T(2,128)S(1)} %copy-done, ...), custom_call_target="tpu_custom_call" | custom-call | tf_op jit(solution)/shard_map/synthesis/pallas_call | solution.py:522
  1.6 15.1 %all_to_all.11 = bf16[32,8,384]{2,1,0:T(8,128)(2,1)S(1)} all-to-all(bf16[32,8,384]{2,1,0:T(8,128)(2,1)S(1)} %bitcast.3), channel_id=1, replica_groups={{29,22,11,28,17,10,31,16,5,30,19,4,25,18,7,24,13,6,27,12,1,26,15,0,21,1..., dimensions={0} | all-to-all | bytes 393216 | tf_op jit(solution)/shard_map/all_to_all | solution.py:537
  16.7 0.5 %products.1 = (bf16[8,384]{1,0:T(8,128)(2,1)S(1)}, bf16[8,384]{1,0:T(8,128)(2,1)S(1)}, bf16[8,384]{1,0:T(8,128)(2,1)S(1)}, bf16[8,384]{1,0:T(8,128)(2,1)S(1)}) custom-call(bf16[256,384]{1,0:T(8,128)(2,1)S(1)} %bitcast.2, bf16[384,256]{1,0:T(8,128)(2,1)S(1)} %get-tuple-element.16.high_ref, bf16[384,256]{1,0:T(8,128)(2,1)S(1)} %get-tuple-element.17.rest_ref, ...), custom_call_target="tpu_custom_call" | custom-call | tf_op jit(solution)/shard_map/products/pallas_call | solution.py:540
  17.2 0.3 %collective-permute-start = (bf16[8,384]{1,0:T(8,128)(2,1)S(1)}, bf16[8,384]{1,0:T(8,128)(2,1)S(1)}, u32[]{:S(2)}, u32[]{:S(2)}) collective-permute-start(bf16[8,384]{1,0:T(8,128)(2,1)S(1)} %get-tuple-element.20), channel_id=1, source_target_pairs={{0,1},{1,0},{2,3},{3,2},{4,5},{5,4},{6,7},{7,6},{8,9},{9,8},{10,11... | collective-permute-start | bytes 18440 | tf_op jit(solution)/shard_map/ppermute | solution.py:551
  17.6 0.7 %collective-permute-start.1 = (bf16[8,384]{1,0:T(8,128)(2,1)S(1)}, bf16[8,384]{1,0:T(8,128)(2,1)S(1)}, u32[]{:S(2)}, u32[]{:S(2)}) collective-permute-start(bf16[8,384]{1,0:T(8,128)(2,1)S(1)} %get-tuple-element.21), channel_id=1, source_target_pairs={{0,8},{1,9},{2,10},{3,11},{4,12},{5,13},{6,14},{7,15},{8,0},{9,1},... | collective-permute-start | bytes 18440 | tf_op jit(solution)/shard_map/ppermute | solution.py:551
  18.3 0.9 %collective-permute-start.2 = (bf16[8,384]{1,0:T(8,128)(2,1)S(1)}, bf16[8,384]{1,0:T(8,128)(2,1)S(1)}, u32[]{:S(2)}, u32[]{:S(2)}) collective-permute-start(bf16[8,384]{1,0:T(8,128)(2,1)S(1)} %get-tuple-element.22), channel_id=1, source_target_pairs={{0,9},{1,8},{2,11},{3,10},{4,13},{5,12},{6,15},{7,14},{8,1},{9,0},... | collective-permute-start | bytes 18440 | tf_op jit(solution)/shard_map/ppermute | solution.py:551
  19.2 0.0 collective-permute-done.refs_1_
  19.2 2.0 %collective-permute-done.1.refs_2_ = bf16[8,384]{1,0:T(8,128)(2,1)S(1)} collective-permute-done((bf16[8,384]{1,0:T(8,128)(2,1)S(1)}, bf16[8,384]{1,0:T(8,128)(2,1)S(1)}, u32[]{:S(2)}, u32[]{:S(2)}) %collective-permute-start.1) | collective-permute-done | bytes 6176 | tf_op jit(solution)/shard_map/ppermute | solution.py:551
  21.2 0.1 collective-permute-done.2.refs_3_
  21.3 0.9 %step.1 = f32[2,3,2,2,129]{4,3,2,1,0:T(2,128)} custom-call(s32[64]{0:T(128)S(1)} %copy-done.1, f32[2,3,8,128]{3,2,1,0:T(8,128)S(1)} %get-tuple-element.14.factor_ref, f32[2,3,2,2,129]{4,3,2,1,0:T(2,128)S(1)} %copy-done, bf16[2,129,128]{2,1,0:T(8,128)(2,1)S(1)} %copy.6.table_ref, bf16[8,384]{1,0:T(8,128)(2,1)S(1)} %get-tuple-element.19.refs_0_, ...), custom_call_target="tpu_custom_call" | custom-call | tf_op jit(solution)/shard_map/step/pallas_call | solution.py:552
Async XLA Ops:
  0.0 1.0 %copy-start.1 = (s32[64]{0:T(128)S(1)}, s32[64]{0:T(128)}, u32[]{:S(2)}) copy-start(s32[64]{0:T(128)} %low_ref.3) | copy-start | bytes 772
  0.0 1.0 %copy-start = (f32[2,3,2,2,129]{4,3,2,1,0:T(2,128)S(1)}, f32[2,3,2,2,129]{4,3,2,1,0:T(2,128)}, u32[]{:S(2)}) copy-start(f32[2,3,2,2,129]{4,3,2,1,0:T(2,128)} %state_ref.3) | copy-start | bytes 37156
  0.0 1.0 %copy-start.3 = (f32[3]{0:T(128)S(1)}, f32[3]{0:T(128)}, u32[]{:S(2)}) copy-start(f32[3]{0:T(128)} %coupling_ref.1) | copy-start | bytes 40
  0.0 1.0 %copy-start.2 = (f32[3]{0:T(128)S(1)}, f32[3]{0:T(128)}, u32[]{:S(2)}) copy-start(f32[3]{0:T(128)} %rate_ref.1) | copy-start | bytes 40
  17.2 1.9 %collective-permute-start = (bf16[8,384]{1,0:T(8,128)(2,1)S(1)}, bf16[8,384]{1,0:T(8,128)(2,1)S(1)}, u32[]{:S(2)}, u32[]{:S(2)}) collective-permute-start(bf16[8,384]{1,0:T(8,128)(2,1)S(1)} %get-tuple-element.20), channel_id=1, source_target_pairs={{0,1},{1,0},{2,3},{3,2},{4,5},{5,4},{6,7},{7,6},{8,9},{9,8},{10,11... | collective-permute-start | bytes 18440 | tf_op jit(solution)/shard_map/ppermute | solution.py:551
  17.6 3.6 %collective-permute-start.1 = (bf16[8,384]{1,0:T(8,128)(2,1)S(1)}, bf16[8,384]{1,0:T(8,128)(2,1)S(1)}, u32[]{:S(2)}, u32[]{:S(2)}) collective-permute-start(bf16[8,384]{1,0:T(8,128)(2,1)S(1)} %get-tuple-element.21), channel_id=1, source_target_pairs={{0,8},{1,9},{2,10},{3,11},{4,12},{5,13},{6,14},{7,15},{8,0},{9,1},... | collective-permute-start | bytes 18440 | tf_op jit(solution)/shard_map/ppermute | solution.py:551
  18.3 3.1 %collective-permute-start.2 = (bf16[8,384]{1,0:T(8,128)(2,1)S(1)}, bf16[8,384]{1,0:T(8,128)(2,1)S(1)}, u32[]{:S(2)}, u32[]{:S(2)}) collective-permute-start(bf16[8,384]{1,0:T(8,128)(2,1)S(1)} %get-tuple-element.22), channel_id=1, source_target_pairs={{0,9},{1,8},{2,11},{3,10},{4,13},{5,12},{6,15},{7,14},{8,1},{9,0},... | collective-permute-start | bytes 18440 | tf_op jit(solution)/shard_map/ppermute | solution.py:551

commit v5 on v4

--- a/solution.py
+++ b/solution.py
@@ -425,8 +425,9 @@
 
 def band_product_kernel(scale, sent_ref, high_ref, rest_ref, own_ref, *out_refs):
     sent = sent_ref[...]
-    grid = jnp.dot(high_ref[...], sent, preferred_element_type=jnp.float32)
-    grid = grid + jnp.dot(rest_ref[...], sent, preferred_element_type=jnp.float32)
+    both = jnp.concatenate([high_ref[...], rest_ref[...]], axis=0)
+    grid = jnp.dot(both, sent, preferred_element_type=jnp.float32)
+    grid = grid[: high_ref.shape[0]] + grid[high_ref.shape[0] :]
     width = sent.shape[1] // 3
     first, second, third = (grid[:, f * width : (f + 1) * width] for f in range(3))
     products = jnp.concatenate([first * second, first * third, second * third], axis=1)

time: 22.4 us -> 22.4 us (level)
  no operation moved by 1% of the time
where the time goes in v5:
time: 22.4 us; the launch traced here: 22.2 us
  blocking collectives  15.1 us (67%)
  waiting for transfers between devices  2.17 us (10%)
  Pallas kernels  1.98 us (9%)
  starting transfers between devices  1.93 us (9%)
  local copies, waits for them, and re-layouts  0.96 us (4%)
    all_to_all x1, blocking collectives, banded(): lax.all_to_all(chunks, 'mode', split_axis=0, concat_axis=0, tiled=True, a...  15.1 us
    ppermute x3, waiting for transfers between devices, banded(): returned.append(lax.ppermute(answers[mask], 'mode', ring))  2.17 us
    ppermute x3, starting transfers between devices, banded(): returned.append(lax.ppermute(answers[mask], 'mode', ring))  1.93 us
    unnamed x9, local copies, waits for them, and re-layouts  0.96 us
    pallas_call x1, Pallas kernels, banded(): pl.pallas_call(functools.partial(band_step_kernel, (group, mode_count, or...  0.89 us
    pallas_call x1, Pallas kernels, banded(): pl.pallas_call(functools.partial(band_synthesis_kernel, (group, mode_coun...  0.56 us
    pallas_call x1, Pallas kernels, banded(): pl.pallas_call(functools.partial(band_product_kernel, scale), out_shape=[...  0.53 us
  transfers between devices with their start and end apart: 3, of which 2 were waited for; matrix products, arithmetic and copies ran while one was open for 0% of the time, Pallas kernels for 0%

profile of v5, /device:TPU:0, one launch (start us, length us, event | category | flops | bytes accessed | tf_op | source)
XLA Modules:
  0.0 22.2 jit_solution(15863001035158546210)
XLA Ops:
  0.0 0.0 copy-start.1
  0.0 0.0 copy-start
  0.0 0.0 copy-start.3
  0.0 0.0 copy-start.2
  0.0 0.9 %copy.6.table_ref = bf16[2,129,128]{2,1,0:T(8,128)(2,1)S(1)} copy(bf16[2,129,128]{2,0,1:T(2,128)(2,1)} %param.6) | data formatting | bytes 132096 | tf_op args[1]
  1.0 0.0 copy-done.1
  1.0 0.0 copy-done
  1.0 0.0 copy-done.3
  1.0 0.0 copy-done.2
  1.0 0.6 %synthesis.1 = (bf16[256,384]{1,0:T(8,128)(2,1)S(1)}, bf16[384,256]{1,0:T(8,128)(2,1)S(1)}, bf16[384,256]{1,0:T(8,128)(2,1)S(1)}, bf16[64,384]{1,0:T(8,128)(2,1)S(1)}, f32[2,3,8,128]{3,2,1,0:T(8,128)S(1)}) custom-call(s32[64]{0:T(128)S(1)} %copy-done.1, f32[3]{0:T(128)S(1)} %copy-done.2, f32[3]{0:T(128)S(1)} %copy-done.3, f32[2,3,2,2,129]{4,3,2,1,0:T(2,128)S(1)} %copy-done, ...), custom_call_target="tpu_custom_call" | custom-call | tf_op jit(solution)/shard_map/synthesis/pallas_call | solution.py:523
  1.6 15.1 %all_to_all.11 = bf16[32,8,384]{2,1,0:T(8,128)(2,1)S(1)} all-to-all(bf16[32,8,384]{2,1,0:T(8,128)(2,1)S(1)} %bitcast.3), channel_id=1, replica_groups={{29,22,11,28,17,10,31,16,5,30,19,4,25,18,7,24,13,6,27,12,1,26,15,0,21,1..., dimensions={0} | all-to-all | bytes 393216 | tf_op jit(solution)/shard_map/all_to_all | solution.py:538
  16.7 0.5 %products.1 = (bf16[8,384]{1,0:T(8,128)(2,1)S(1)}, bf16[8,384]{1,0:T(8,128)(2,1)S(1)}, bf16[8,384]{1,0:T(8,128)(2,1)S(1)}, bf16[8,384]{1,0:T(8,128)(2,1)S(1)}) custom-call(bf16[256,384]{1,0:T(8,128)(2,1)S(1)} %bitcast.2, bf16[384,256]{1,0:T(8,128)(2,1)S(1)} %get-tuple-element.16.high_ref, bf16[384,256]{1,0:T(8,128)(2,1)S(1)} %get-tuple-element.17.rest_ref, ...), custom_call_target="tpu_custom_call" | custom-call | tf_op jit(solution)/shard_map/products/pallas_call | solution.py:541
  17.2 0.3 %collective-permute-start = (bf16[8,384]{1,0:T(8,128)(2,1)S(1)}, bf16[8,384]{1,0:T(8,128)(2,1)S(1)}, u32[]{:S(2)}, u32[]{:S(2)}) collective-permute-start(bf16[8,384]{1,0:T(8,128)(2,1)S(1)} %get-tuple-element.20), channel_id=1, source_target_pairs={{0,1},{1,0},{2,3},{3,2},{4,5},{5,4},{6,7},{7,6},{8,9},{9,8},{10,11... | collective-permute-start | bytes 18440 | tf_op jit(solution)/shard_map/ppermute | solution.py:552
  17.6 0.7 %collective-permute-start.1 = (bf16[8,384]{1,0:T(8,128)(2,1)S(1)}, bf16[8,384]{1,0:T(8,128)(2,1)S(1)}, u32[]{:S(2)}, u32[]{:S(2)}) collective-permute-start(bf16[8,384]{1,0:T(8,128)(2,1)S(1)} %get-tuple-element.21), channel_id=1, source_target_pairs={{0,8},{1,9},{2,10},{3,11},{4,12},{5,13},{6,14},{7,15},{8,0},{9,1},... | collective-permute-start | bytes 18440 | tf_op jit(solution)/shard_map/ppermute | solution.py:552
  18.3 0.9 %collective-permute-start.2 = (bf16[8,384]{1,0:T(8,128)(2,1)S(1)}, bf16[8,384]{1,0:T(8,128)(2,1)S(1)}, u32[]{:S(2)}, u32[]{:S(2)}) collective-permute-start(bf16[8,384]{1,0:T(8,128)(2,1)S(1)} %get-tuple-element.22), channel_id=1, source_target_pairs={{0,9},{1,8},{2,11},{3,10},{4,13},{5,12},{6,15},{7,14},{8,1},{9,0},... | collective-permute-start | bytes 18440 | tf_op jit(solution)/shard_map/ppermute | solution.py:552
  19.2 0.0 collective-permute-done.refs_1_
  19.2 2.0 %collective-permute-done.1.refs_2_ = bf16[8,384]{1,0:T(8,128)(2,1)S(1)} collective-permute-done((bf16[8,384]{1,0:T(8,128)(2,1)S(1)}, bf16[8,384]{1,0:T(8,128)(2,1)S(1)}, u32[]{:S(2)}, u32[]{:S(2)}) %collective-permute-start.1) | collective-permute-done | bytes 6176 | tf_op jit(solution)/shard_map/ppermute | solution.py:552
  21.2 0.1 collective-permute-done.2.refs_3_
  21.3 0.9 %step.1 = f32[2,3,2,2,129]{4,3,2,1,0:T(2,128)} custom-call(s32[64]{0:T(128)S(1)} %copy-done.1, f32[2,3,8,128]{3,2,1,0:T(8,128)S(1)} %get-tuple-element.14.factor_ref, f32[2,3,2,2,129]{4,3,2,1,0:T(2,128)S(1)} %copy-done, bf16[2,129,128]{2,1,0:T(8,128)(2,1)S(1)} %copy.6.table_ref, bf16[8,384]{1,0:T(8,128)(2,1)S(1)} %get-tuple-element.19.refs_0_, ...), custom_call_target="tpu_custom_call" | custom-call | tf_op jit(solution)/shard_map/step/pallas_call | solution.py:553
Async XLA Ops:
  0.0 1.0 %copy-start.1 = (s32[64]{0:T(128)S(1)}, s32[64]{0:T(128)}, u32[]{:S(2)}) copy-start(s32[64]{0:T(128)} %low_ref.3) | copy-start | bytes 772
  0.0 1.0 %copy-start = (f32[2,3,2,2,129]{4,3,2,1,0:T(2,128)S(1)}, f32[2,3,2,2,129]{4,3,2,1,0:T(2,128)}, u32[]{:S(2)}) copy-start(f32[2,3,2,2,129]{4,3,2,1,0:T(2,128)} %state_ref.3) | copy-start | bytes 37156
  0.0 1.0 %copy-start.3 = (f32[3]{0:T(128)S(1)}, f32[3]{0:T(128)}, u32[]{:S(2)}) copy-start(f32[3]{0:T(128)} %coupling_ref.1) | copy-start | bytes 40
  0.0 1.0 %copy-start.2 = (f32[3]{0:T(128)S(1)}, f32[3]{0:T(128)}, u32[]{:S(2)}) copy-start(f32[3]{0:T(128)} %rate_ref.1) | copy-start | bytes 40
  17.2 1.9 %collective-permute-start = (bf16[8,384]{1,0:T(8,128)(2,1)S(1)}, bf16[8,384]{1,0:T(8,128)(2,1)S(1)}, u32[]{:S(2)}, u32[]{:S(2)}) collective-permute-start(bf16[8,384]{1,0:T(8,128)(2,1)S(1)} %get-tuple-element.20), channel_id=1, source_target_pairs={{0,1},{1,0},{2,3},{3,2},{4,5},{5,4},{6,7},{7,6},{8,9},{9,8},{10,11... | collective-permute-start | bytes 18440 | tf_op jit(solution)/shard_map/ppermute | solution.py:552
  17.6 3.6 %collective-permute-start.1 = (bf16[8,384]{1,0:T(8,128)(2,1)S(1)}, bf16[8,384]{1,0:T(8,128)(2,1)S(1)}, u32[]{:S(2)}, u32[]{:S(2)}) collective-permute-start(bf16[8,384]{1,0:T(8,128)(2,1)S(1)} %get-tuple-element.21), channel_id=1, source_target_pairs={{0,8},{1,9},{2,10},{3,11},{4,12},{5,13},{6,14},{7,15},{8,0},{9,1},... | collective-permute-start | bytes 18440 | tf_op jit(solution)/shard_map/ppermute | solution.py:552
  18.3 3.1 %collective-permute-start.2 = (bf16[8,384]{1,0:T(8,128)(2,1)S(1)}, bf16[8,384]{1,0:T(8,128)(2,1)S(1)}, u32[]{:S(2)}, u32[]{:S(2)}) collective-permute-start(bf16[8,384]{1,0:T(8,128)(2,1)S(1)} %get-tuple-element.22), channel_id=1, source_target_pairs={{0,9},{1,8},{2,11},{3,10},{4,13},{5,12},{6,15},{7,14},{8,1},{9,0},... | collective-permute-start | bytes 18440 | tf_op jit(solution)/shard_map/ppermute | solution.py:552
